TPU v7x, 32 devices: a whole 2x2x4 slice. The times are simulated.
32 devices in a mesh: dp: 8 (over y, x, core), seq: 4 (over z).
Axes of the slice: x: 2, y: 2, z: 4, core: 2. Of those that a mesh axis runs over, the one named last changes fastest.
Arguments:
- queries: bfloat16 [4096, 4096], P(('dp', 'seq')), may hold values from -300 to 300
- key_proj: bfloat16 [4096, 512], P(('dp', 'seq')), may hold values from -4.5 to 4.5
- value_proj: bfloat16 [4096, 512], P(('dp', 'seq')), may hold values from -6 to 6
- seq_lengths: int32 [32], replicated, may hold values from 1 to 257, 4096 in all
Outputs:
- attended: bfloat16 [4096, 4096], P(('dp', 'seq'))
Inputs may be any that keep to these rules, and one draw needn't show every extreme that they name: `seq_lengths`: the sequences cover all 4096 tokens; the longest has exactly 257 tokens.
All inputs are finite; a program needn't handle non-finite values.
Results may differ from a plain program's by a relative error of at most 0.0036.
Values may be sent and summed in bfloat16 or wider, within the bound.
No kernel may reach another device: no remote copies, remote signals or barrier semaphores. Data moves between devices by JAX's collectives and lax.ppermute only.
A program may use at most 64 MiB of HBM per device.

v0:
```python
import math

import jax
import jax.numpy as jnp
from jax import lax
from jax.sharding import PartitionSpec as P

HD = 128
QH = 32
KVH = 4


score_scale = 0.08838834764831845
neg_fill = -1e30


def from_behind(block, axis, distance):
    devices = range(lax.axis_size(axis))
    route = [(i - distance, i) for i in devices if i - distance in devices]
    return lax.ppermute(block, axis, route)


def segment_starts(seq_lengths, positions):
    seq_ends = jnp.cumsum(seq_lengths)
    begins = seq_ends - seq_lengths
    covered = begins[None, :] <= positions[:, None]
    return jnp.max(jnp.where(covered, begins[None, :], 0), axis=1)


def attend(
    queries,
    own_keys,
    own_values,
    tail_keys,
    tail_values,
    query_pos,
    key_pos,
    tail_pos,
    query_start,
    tail_limit,
):
    row_count = queries.shape[0]
    heads_query = queries.shape[1]
    group_size = heads_query // own_keys.shape[1]
    tile_rows = math.gcd(row_count, 512)
    tail_count = tail_keys.shape[0]
    pieces = []
    for offset in range(0, row_count, tile_rows):
        query_tile = queries[offset : offset + tile_rows]
        pos_tile = query_pos[offset : offset + tile_rows]
        start_tile = query_start[offset : offset + tile_rows]
        key_count = offset + tile_rows
        keys_used = own_keys[:key_count]
        values_used = own_values[:key_count]
        pos_used = key_pos[:key_count]
        own_mask = (pos_used[None, :] <= pos_tile[:, None]) & (
            pos_used[None, :] >= start_tile[:, None]
        )
        use_tail = offset < tail_limit
        tail_mask = tail_pos[None, :] >= start_tile[:, None]
        reached = jnp.any(tail_mask)

        def one_head(head_index):
            shared_index = head_index // group_size
            query_head = lax.dynamic_index_in_dim(query_tile, head_index, 1, keepdims=False)
            key_head = lax.dynamic_index_in_dim(keys_used, shared_index, 1, keepdims=False)
            value_head = lax.dynamic_index_in_dim(values_used, shared_index, 1, keepdims=False)
            own_scores = (
                jnp.einsum("qd,kd->qk", query_head, key_head, preferred_element_type=jnp.float32)
                * score_scale
            )
            own_scores = jnp.where(own_mask, own_scores, neg_fill)
            row_max = jnp.max(own_scores, axis=1)
            if use_tail:
                tail_key = lax.dynamic_index_in_dim(tail_keys, shared_index, 1, keepdims=False)
                tail_value = lax.dynamic_index_in_dim(tail_values, shared_index, 1, keepdims=False)

                def tail_scores_fn():
                    raw = (
                        jnp.einsum(
                            "qd,kd->qk", query_head, tail_key, preferred_element_type=jnp.float32
                        )
                        * score_scale
                    )
                    return jnp.where(tail_mask, raw, neg_fill)

                def tail_empty():
                    return jnp.full((tile_rows, tail_count), neg_fill, jnp.float32)

                tail_scores = lax.cond(reached, tail_scores_fn, tail_empty)
                row_max = jnp.maximum(row_max, jnp.max(tail_scores, axis=1))
            own_weights = jnp.where(own_mask, jnp.exp(own_scores - row_max[:, None]), 0.0)
            row_sum = jnp.sum(own_weights, axis=1)
            weighted = jnp.dot(
                own_weights.astype(jnp.bfloat16), value_head, preferred_element_type=jnp.float32
            )
            if use_tail:
                tail_weights = jnp.where(tail_mask, jnp.exp(tail_scores - row_max[:, None]), 0.0)
                row_sum = row_sum + jnp.sum(tail_weights, axis=1)

                def tail_product():
                    return jnp.dot(
                        tail_weights.astype(jnp.bfloat16),
                        tail_value,
                        preferred_element_type=jnp.float32,
                    )

                def tail_zero():
                    return jnp.zeros((tile_rows, value_head.shape[1]), jnp.float32)

                weighted = weighted + lax.cond(reached, tail_product, tail_zero)
            return (weighted / row_sum[:, None]).astype(jnp.bfloat16)

        per_head = lax.map(one_head, jnp.arange(heads_query, dtype=jnp.int32))
        pieces.append(jnp.transpose(per_head, (1, 0, 2)))
    return jnp.concatenate(pieces, axis=0)


def body(queries, key_proj, value_proj, seq_lengths):
    tok_rows = queries.shape[0]
    members = lax.axis_size("seq")
    home_index = lax.axis_index("dp")
    block_rows = tok_rows * members
    reach_rows = block_rows // 2
    block_start = home_index * block_rows
    key_pos = block_start + jnp.arange(block_rows, dtype=jnp.int32)
    tail_pos = block_start - reach_rows + jnp.arange(reach_rows, dtype=jnp.int32)
    local_heads = QH // members
    copies = max(1, members // KVH)
    query_split = queries.reshape(tok_rows, members, local_heads * HD)
    key_split = key_proj.reshape(tok_rows, KVH, HD)
    value_split = value_proj.reshape(tok_rows, KVH, HD)
    if copies > 1:
        key_split = jnp.repeat(key_split, copies, axis=1)
        value_split = jnp.repeat(value_split, copies, axis=1)
    query_block, key_block, value_block = (
        lax.all_to_all(query_split, "seq", split_axis=1, concat_axis=0, tiled=True),
        lax.all_to_all(key_split, "seq", split_axis=1, concat_axis=0, tiled=True),
        lax.all_to_all(value_split, "seq", split_axis=1, concat_axis=0, tiled=True),
    )
    query_block = query_block.reshape(block_rows, local_heads, HD)
    tail_keys, tail_values = from_behind(
        (key_block[reach_rows:], value_block[reach_rows:]), "dp", 1
    )
    starts = segment_starts(seq_lengths, key_pos)
    mixed = attend(
        query_block,
        key_block,
        value_block,
        tail_keys,
        tail_values,
        key_pos,
        key_pos,
        tail_pos,
        starts,
        reach_rows,
    )
    mixed = mixed.reshape(block_rows, 1, local_heads * HD)
    returned = lax.all_to_all(mixed, "seq", split_axis=0, concat_axis=1, tiled=True)
    return returned.reshape(tok_rows, QH * HD)


def solution(mesh):
    return jax.shard_map(
        body,
        mesh=mesh,
        in_specs=(P(("dp", "seq"), None), P(("dp", "seq"), None), P(("dp", "seq"), None), P()),
        out_specs=P(("dp", "seq"), None),
        check_vma=False,
    )
```

profile of v0, /device:TPU:4, one launch (start us, length us, event | category | flops | bytes accessed | tf_op | source)
XLA Modules:
  0.0 136.4 jit_solution(15620430314450670122)
XLA Ops:
  0.0 1.7 %copy.50 = bf16[128,512]{0,1:T(8,128)(2,1)} copy(bf16[128,512]{1,0:T(8,128)(2,1)} %param.11) | data formatting | bytes 262144 | tf_op args[1]
  1.7 4.9 %all-to-all-start.1 = ((bf16[128,4,128]{0,2,1:T(8,128)(2,1)}), bf16[128,4,128]{0,2,1:T(8,128)(2,1)S(1)}, u32[]{:S(2)}, u32[]{:S(2)}) async-start(bf16[128,4,128]{0,2,1:T(8,128)(2,1)} %bitcast.5), calls=%async_computation.1 | async-start | bytes 262144 | tf_op jit(solution)/shard_map/all_to_all | solution.py:138
  6.5 1.7 %copy.54 = bf16[128,512]{0,1:T(8,128)(2,1)} copy(bf16[128,512]{1,0:T(8,128)(2,1)} %param.12) | data formatting | bytes 262144 | tf_op args[2]
  8.2 4.4 %all-to-all-done.1 = bf16[128,4,128]{0,2,1:T(8,128)(2,1)S(1)} async-done(((bf16[128,4,128]{0,2,1:T(8,128)(2,1)}), bf16[128,4,128]{0,2,1:T(8,128)(2,1)S(1)}, u32[]{:S(2)}, u32[]{:S(2)}) %all-to-all-start.1) | async-done | bytes 131104 | tf_op jit(solution)/shard_map/all_to_all | solution.py:138
  12.6 3.3 %all-to-all-start.2 = ((bf16[128,4,128]{0,2,1:T(8,128)(2,1)}), bf16[128,4,128]{0,2,1:T(8,128)(2,1)S(1)}, u32[]{:S(2)}, u32[]{:S(2)}) async-start(bf16[128,4,128]{0,2,1:T(8,128)(2,1)} %bitcast.12), calls=%async_computation.2 | async-start | bytes 262144 | tf_op jit(solution)/shard_map/all_to_all | solution.py:139
  16.0 2.3 %copy.70 = bf16[16,4,8,1024]{3,2,0,1:T(8,128)(2,1)} copy(bf16[16,4,8,1024]{3,2,1,0:T(8,128)(2,1)} %bitcast.80) | data formatting | bytes 2097152 | tf_op jit(solution)/shard_map/reshape | solution.py:130
  18.3 3.6 %all-to-all-done.2 = bf16[128,4,128]{0,2,1:T(8,128)(2,1)S(1)} async-done(((bf16[128,4,128]{0,2,1:T(8,128)(2,1)}), bf16[128,4,128]{0,2,1:T(8,128)(2,1)S(1)}, u32[]{:S(2)}, u32[]{:S(2)}) %all-to-all-start.2) | async-done | bytes 131104 | tf_op jit(solution)/shard_map/all_to_all | solution.py:139
  21.8 3.5 %all-to-all-start = ((bf16[128,4,1024]{2,0,1:T(8,128)(2,1)}), bf16[128,4,1024]{2,0,1:T(8,128)(2,1)S(1)}, u32[]{:S(2)}, u32[]{:S(2)}) async-start(bf16[128,4,1024]{2,0,1:T(8,128)(2,1)} %bitcast.58), calls=%async_computation | async-start | bytes 2097152 | tf_op jit(solution)/shard_map/all_to_all | solution.py:137
  25.9 1.9 %collective-permute-start = (bf16[256,1,128]{2,0,1:T(8,128)(2,1)S(1)}, bf16[256,1,128]{2,0,1:T(8,128)(2,1)S(1)}, u32[]{:S(2)}, u32[]{:S(2)}) collective-permute-start(bf16[256,1,128]{2,0,1:T(8,128)(2,1)S(1)} %bitcast.91), channel_id=1, source_target_pairs={{0,4},{4,8},{8,12},{12,16},{16,20},{20,24},{24,28},{1,5},{5,9},{9,... | collective-permute-start | bytes 196616 | tf_op jit(solution)/shard_map/ppermute | solution.py:20
  28.0 3.5 %collective-permute-start.1 = (bf16[256,1,128]{2,0,1:T(8,128)(2,1)S(1)}, bf16[256,1,128]{2,0,1:T(8,128)(2,1)S(1)}, u32[]{:S(2)}, u32[]{:S(2)}) collective-permute-start(bf16[256,1,128]{2,0,1:T(8,128)(2,1)S(1)} %bitcast.92), channel_id=1, source_target_pairs={{0,4},{4,8},{8,12},{12,16},{16,20},{20,24},{24,28},{1,5},{5,9},{9,... | collective-permute-start | bytes 196616 | tf_op jit(solution)/shard_map/ppermute | solution.py:20
  31.5 0.9 compare_reduce_fusion
  32.6 16.2 %all-to-all-done = bf16[128,4,1024]{2,0,1:T(8,128)(2,1)S(1)} async-done(((bf16[128,4,1024]{2,0,1:T(8,128)(2,1)}), bf16[128,4,1024]{2,0,1:T(8,128)(2,1)S(1)}, u32[]{:S(2)}, u32[]{:S(2)}) %all-to-all-start) | async-done | bytes 1048608 | tf_op jit(solution)/shard_map/all_to_all | solution.py:137
  49.2 51.4 %while.12 = (s32[]{:T(128)}, bf16[8,512,128]{1,2,0:T(8,128)(2,1)}, s32[8]{0:T(128)S(1)}, bf16[512,8,128]{2,0,1:T(8,128)(2,1)S(1)}, bf16[512,1,128]{2,0,1:T(8,128...) while((s32[]{:T(128)}, bf16[8,512,128]{1,2,0:T(8,128)(2,1)}, ...), condition=%wide.region_12.13_spmd.clone.clone, body=%wide.region_3.12_spmd.clone.clone.sunk | while | flops 207420416 | bytes 8435984 | solution.py:114
  52.4 0.7 conditional.8
  55.0 0.7 constant_dynamic-update-slice_fusion.2
  58.8 0.7 conditional.8
  61.4 0.7 constant_dynamic-update-slice_fusion.2
  65.2 0.7 conditional.8
  67.9 0.7 constant_dynamic-update-slice_fusion.2
  71.7 0.7 conditional.8
  74.3 0.7 constant_dynamic-update-slice_fusion.2
  78.1 0.7 conditional.8
  80.7 0.7 constant_dynamic-update-slice_fusion.2
  84.5 0.7 conditional.8
  87.1 0.7 constant_dynamic-update-slice_fusion.2
  90.9 0.7 conditional.8
  97.4 0.7 conditional.8
  101.2 2.7 %reduce.1 = bf16[512,1024]{0,1:T(8,128)(2,1)S(1)} reduce(bf16[512,1,1024]{0,2,1:T(8,128)(2,1)} %bitcast.79, bf16[]{:T(256)} %broadcast.33), dimensions={1}, to_apply=%copy.59.reduce_sub_computation | reduce | bytes 2097154 | tf_op jit(solution)/shard_map/reshape | solution.py:158
  104.5 0.8 reshape.80
  105.3 27.7 %all_to_all.66 = bf16[4,2,65536]{2,1,0:T(2,128)(2,1)S(1)} all-to-all(bf16[4,2,65536]{2,1,0:T(2,128)(2,1)S(1)} %reshape.80), channel_id=1, replica_groups=mesh['dp'=8,'seq'=4] {'seq'}, dimensions={0} | all-to-all | bytes 2097152 | tf_op jit(solution)/shard_map/all_to_all | solution.py:159
  133.0 0.9 reshape.81
  135.0 1.3 copy.61
  (147 shorter events, 32.7 us)
Async XLA Ops:
  1.7 10.9 %all-to-all-start.1 = ((bf16[128,4,128]{0,2,1:T(8,128)(2,1)}), bf16[128,4,128]{0,2,1:T(8,128)(2,1)S(1)}, u32[]{:S(2)}, u32[]{:S(2)}) async-start(bf16[128,4,128]{0,2,1:T(8,128)(2,1)} %bitcast.5), calls=%async_computation.1 | async-start | bytes 262144 | tf_op jit(solution)/shard_map/all_to_all | solution.py:138
  12.6 9.2 %all-to-all-start.2 = ((bf16[128,4,128]{0,2,1:T(8,128)(2,1)}), bf16[128,4,128]{0,2,1:T(8,128)(2,1)S(1)}, u32[]{:S(2)}, u32[]{:S(2)}) async-start(bf16[128,4,128]{0,2,1:T(8,128)(2,1)} %bitcast.12), calls=%async_computation.2 | async-start | bytes 262144 | tf_op jit(solution)/shard_map/all_to_all | solution.py:139
  15.9 9.4 %copy-start = (s32[32]{0:T(128)S(1)}, s32[32]{0:T(128)}, u32[]{:S(2)}) copy-start(s32[32]{0:T(128)} %param.13) | copy-start | bytes 388
  21.8 27.0 %all-to-all-start = ((bf16[128,4,1024]{2,0,1:T(8,128)(2,1)}), bf16[128,4,1024]{2,0,1:T(8,128)(2,1)S(1)}, u32[]{:S(2)}, u32[]{:S(2)}) async-start(bf16[128,4,1024]{2,0,1:T(8,128)(2,1)} %bitcast.58), calls=%async_computation | async-start | bytes 2097152 | tf_op jit(solution)/shard_map/all_to_all | solution.py:137
  25.9 23.3 %collective-permute-start = (bf16[256,1,128]{2,0,1:T(8,128)(2,1)S(1)}, bf16[256,1,128]{2,0,1:T(8,128)(2,1)S(1)}, u32[]{:S(2)}, u32[]{:S(2)}) collective-permute-start(bf16[256,1,128]{2,0,1:T(8,128)(2,1)S(1)} %bitcast.91), channel_id=1, source_target_pairs={{0,4},{4,8},{8,12},{12,16},{16,20},{20,24},{24,28},{1,5},{5,9},{9,... | collective-permute-start | bytes 196616 | tf_op jit(solution)/shard_map/ppermute | solution.py:20
  28.0 21.3 %collective-permute-start.1 = (bf16[256,1,128]{2,0,1:T(8,128)(2,1)S(1)}, bf16[256,1,128]{2,0,1:T(8,128)(2,1)S(1)}, u32[]{:S(2)}, u32[]{:S(2)}) collective-permute-start(bf16[256,1,128]{2,0,1:T(8,128)(2,1)S(1)} %bitcast.92), channel_id=1, source_target_pairs={{0,4},{4,8},{8,12},{12,16},{16,20},{20,24},{24,28},{1,5},{5,9},{9,... | collective-permute-start | bytes 196616 | tf_op jit(solution)/shard_map/ppermute | solution.py:20
where the time goes:
time: 137 us; the launch traced here: 136 us
  blocking collectives  27.7 us (20%)
  local copies, waits for them, and re-layouts  26.2 us (19%)
  waiting for transfers between devices  24.2 us (18%)
  loops' own time  20 us (15%)
  starting transfers between devices  17.1 us (12%)
  matrix products  10.9 us (8%)
  other arithmetic  10 us (7%)
    all_to_all x1, blocking collectives, body(): lax.all_to_all(mixed, 'seq', split_axis=0, concat_axis=1, tiled=True)  27.7 us
    another operation x1, loops' own time, attend(): per_head = lax.map(one_head, jnp.arange(heads_query, dtype=jnp.int32))  19.6 us
    all_to_all x1, waiting for transfers between devices, body(): lax.all_to_all(query_split, 'seq', split_axis=1, concat_axis=0, tiled=True)  16.2 us
    unnamed x10, local copies, waits for them, and re-layouts  6.39 us
    dynamic_update_slice x16, local copies, waits for them, and re-layouts, attend(): per_head = lax.map(one_head, jnp.arange(heads_query, dtype=jnp.int32))  6.27 us
    ppermute x2, starting transfers between devices, from_behind(): return lax.ppermute(block, axis, route)  5.42 us
    all_to_all x1, starting transfers between devices, body(): lax.all_to_all(key_split, 'seq', split_axis=1, concat_axis=0, tiled=True)  4.87 us
    dynamic_slice x8, local copies, waits for them, and re-layouts, attend(): per_head = lax.map(one_head, jnp.arange(heads_query, dtype=jnp.int32))  4.64 us
  transfers between devices with their start and end apart: 5, of which 3 were waited for; matrix products, arithmetic and copies ran while one was open for 4% of the time, Pallas kernels for 0%

commit v1 on v0

v1 whole, which is shorter than its diff:
```python
import functools
import math

import jax
import jax.numpy as jnp
from jax import lax
from jax.experimental import pallas as pl
from jax.experimental.pallas import tpu as pltpu
from jax.sharding import PartitionSpec as P

HD = 128

AXES = ("dp", "seq")
score_scale = 0.08838834764831845
neg_fill = -1e30


def from_behind(block, distance):
    count = lax.axis_size(AXES)
    return lax.ppermute(block, AXES, [(i, i + distance) for i in range(count - distance)])


def attend_kernel(chunks, group, lengths_ref, q_ref, *refs):
    key_refs = refs[:chunks]
    value_refs = refs[chunks : 2 * chunks]
    out_ref, bias_ref, value_ref = refs[2 * chunks :]
    rows = q_ref.shape[0]
    span = chunks * rows

    @pl.when(pl.program_id(0) == 0)
    def _():
        first = lax.axis_index(AXES) * rows
        key_pos = lax.broadcasted_iota(jnp.int32, (8, span), 1) + (first - span + rows)

        def step(i, carry):
            end, last = carry
            end = end + lengths_ref[i]
            return end, jnp.where(key_pos < end, jnp.minimum(last, end - 1), last)

        top = jnp.full((8, span), jnp.iinfo(jnp.int32).max, jnp.int32)
        _, last = lax.fori_loop(0, lengths_ref.shape[0], step, (jnp.int32(0), top), unroll=4)
        last = jnp.where(key_pos < 0, -1, last)
        query_pos = lax.broadcasted_iota(jnp.int32, (rows, span), 0) + first
        allowed = (query_pos >= key_pos[:1]) & (query_pos <= last[:1])
        bias_ref[...] = jnp.where(allowed, 0.0, neg_fill)
        value_ref[:, HD:] = jnp.ones((span, HD), value_ref.dtype)

    keys = jnp.concatenate([ref[...] for ref in key_refs], axis=0)
    for i, ref in enumerate(value_refs):
        value_ref[i * rows : (i + 1) * rows, :HD] = ref[...]
    values = value_ref[...]
    bias = bias_ref[...]
    for head in range(group):
        at = slice(head * HD, (head + 1) * HD)
        scores = lax.dot_general(
            q_ref[:, at], keys, (((1,), (1,)), ((), ())), preferred_element_type=jnp.float32
        )
        scores = scores + bias
        row_max = jnp.max(scores, axis=1, keepdims=True)
        weights = jnp.exp2((scores - row_max) * (score_scale * math.log2(math.e)))
        mixed = jnp.dot(weights.astype(jnp.bfloat16), values, preferred_element_type=jnp.float32)
        out_ref[:, at] = (mixed[:, :HD] / mixed[:, HD:]).astype(out_ref.dtype)


def attend(queries, keys, values, seq_lengths):
    rows = queries.shape[0]
    chunks = len(keys)
    shared = keys[0].shape[1] // HD
    group = queries.shape[1] // keys[0].shape[1]
    wide = pl.BlockSpec((rows, group * HD), lambda h: (0, h))
    narrow = pl.BlockSpec((rows, HD), lambda h: (0, h))
    return pl.pallas_call(
        functools.partial(attend_kernel, chunks, group),
        grid=(shared,),
        in_specs=[pl.BlockSpec(memory_space=pltpu.SMEM), wide] + [narrow] * (2 * chunks),
        out_specs=wide,
        out_shape=jax.ShapeDtypeStruct(queries.shape, queries.dtype),
        scratch_shapes=[
            pltpu.VMEM((rows, chunks * rows), jnp.float32),
            pltpu.VMEM((chunks * rows, 2 * HD), jnp.bfloat16),
        ],
        name="attend",
    )(seq_lengths, queries, *keys, *values)


def body(queries, key_proj, value_proj, seq_lengths):
    rows = queries.shape[0]
    reach = rows * lax.axis_size("seq") // 2
    behind = -(-reach // rows)
    keys, values = [key_proj], [value_proj]
    for distance in range(1, behind + 1):
        keys.insert(0, from_behind(key_proj, distance))
        values.insert(0, from_behind(value_proj, distance))
    return attend(queries, keys, values, seq_lengths)


def solution(mesh):
    return jax.shard_map(
        body,
        mesh=mesh,
        in_specs=(P(AXES, None), P(AXES, None), P(AXES, None), P()),
        out_specs=P(AXES, None),
        check_vma=False,
    )
```

time: 137 us -> 31.5 us (0.23)
  blocking collectives: 27.7 us -> 0 us
  local copies, waits for them, and re-layouts: 26.2 us -> 1.29 us
  loops' own time: 20 us -> 0 us
  waiting for transfers between devices: 24.2 us -> 10.2 us
  matrix products: 10.9 us -> 0 us
  other arithmetic: 10 us -> 0 us
  Pallas kernels: 0 us -> 6.02 us
  starting transfers between devices: 17.1 us -> 13.8 us
    all_to_all x1 -> x0, blocking collectives: 27.7 us -> none  [body(): lax.all_to_all(mixed, 'seq', split_axis=0, concat_axis=1, tiled=True)]
    all_to_all x3 -> x0, waiting for transfers between devices: 24.1 us -> none  [the longest x1 16.2 us: body(): lax.all_to_all(query_split, 'seq', split_axis=1, concat_axis=0, tiled=True)]
    another operation x17 -> x0, loops' own time: 20 us -> none  [the longest x1 19.6 us: attend(): per_head = lax.map(one_head, jnp.arange(heads_query, dtype=jnp.int32))]
    all_to_all x3 -> x0, starting transfers between devices: 11.7 us -> none  [the longest x1 4.87 us: body(): lax.all_to_all(key_split, 'seq', split_axis=1, concat_axis=0, tiled=True)]
    dot_general x32 -> x0, matrix products: 10.9 us -> none  [the longest x8 4.14 us: one_head(): jnp.dot(own_weights.astype(jnp.bfloat16), value_head, preferred_element_t...]
    ppermute x2 -> x4, waiting for transfers between devices: 0.01 us -> 10.2 us  [from_behind(): lax.ppermute(block, AXES, [(i, i + distance) for i in range(count - dista...]
    ppermute x2 -> x4, starting transfers between devices: 5.42 us -> 13.8 us  [from_behind(): lax.ppermute(block, AXES, [(i, i + distance) for i in range(count - dista...]
    dynamic_update_slice x16 -> x0, local copies, waits for them, and re-layouts: 6.27 us -> none  [attend(): per_head = lax.map(one_head, jnp.arange(heads_query, dtype=jnp.int32))]
  transfers between devices with their start and end apart: 5 -> 4, of which waited for: 3 -> 2; matrix products, arithmetic and copies ran while one was open for 4% -> 0% of each run, Pallas kernels for 0% -> 0%
where the time goes in v1:
time: 31.5 us; the launch traced here: 31.3 us
  starting transfers between devices  13.8 us (44%)
  waiting for transfers between devices  10.2 us (32%)
  Pallas kernels  6.02 us (19%)
  local copies, waits for them, and re-layouts  1.29 us (4%)
    ppermute x4, starting transfers between devices, from_behind(): lax.ppermute(block, AXES, [(i, i + distance) for i in range(count - dista...  13.8 us
    ppermute x4, waiting for transfers between devices, from_behind(): lax.ppermute(block, AXES, [(i, i + distance) for i in range(count - dista...  10.2 us
    pallas_call x1, Pallas kernels, attend(): pl.pallas_call(functools.partial(attend_kernel, chunks, group), grid=(sha...  6.02 us
    unnamed x8, local copies, waits for them, and re-layouts  1.29 us
  transfers between devices with their start and end apart: 4, of which 2 were waited for; matrix products, arithmetic and copies ran while one was open for 0% of the time, Pallas kernels for 0%

profile of v1, /device:TPU:4, one launch (start us, length us, event | category | flops | bytes accessed | tf_op | source)
XLA Modules:
  0.0 31.3 jit_solution(16419582849821830974)
XLA Ops:
  0.0 4.5 %collective-permute-start = (bf16[128,512]{1,0:T(8,128)(2,1)}, bf16[128,512]{1,0:T(8,128)(2,1)S(1)}, u32[]{:S(2)}, u32[]{:S(2)}) collective-permute-start(bf16[128,512]{1,0:T(8,128)(2,1)} %refs_2_.1), channel_id=1, source_target_pairs={{0,2},{1,3},{2,4},{3,5},{4,6},{5,7},{6,8},{7,9},{8,10},{9,11},{10,... | collective-permute-start | bytes 393224 | tf_op jit(solution)/shard_map/ppermute | solution.py:20
  4.5 3.5 %collective-permute-start.1 = (bf16[128,512]{1,0:T(8,128)(2,1)}, bf16[128,512]{1,0:T(8,128)(2,1)S(1)}, u32[]{:S(2)}, u32[]{:S(2)}) collective-permute-start(bf16[128,512]{1,0:T(8,128)(2,1)} %refs_2_.1), channel_id=1, source_target_pairs={{0,1},{1,2},{2,3},{3,4},{4,5},{5,6},{6,7},{7,8},{8,9},{9,10},{10,1... | collective-permute-start | bytes 393224 | tf_op jit(solution)/shard_map/ppermute | solution.py:20
  8.0 1.9 %collective-permute-start.2 = (bf16[128,512]{1,0:T(8,128)(2,1)}, bf16[128,512]{1,0:T(8,128)(2,1)S(1)}, u32[]{:S(2)}, u32[]{:S(2)}) collective-permute-start(bf16[128,512]{1,0:T(8,128)(2,1)} %refs_5_.1), channel_id=1, source_target_pairs={{0,2},{1,3},{2,4},{3,5},{4,6},{5,7},{6,8},{7,9},{8,10},{9,11},{10,... | collective-permute-start | bytes 393224 | tf_op jit(solution)/shard_map/ppermute | solution.py:20
  9.9 3.9 %collective-permute-start.3 = (bf16[128,512]{1,0:T(8,128)(2,1)}, bf16[128,512]{1,0:T(8,128)(2,1)S(1)}, u32[]{:S(2)}, u32[]{:S(2)}) collective-permute-start(bf16[128,512]{1,0:T(8,128)(2,1)} %refs_5_.1), channel_id=1, source_target_pairs={{0,1},{1,2},{2,3},{3,4},{4,5},{5,6},{6,7},{7,8},{8,9},{9,10},{10,1... | collective-permute-start | bytes 393224 | tf_op jit(solution)/shard_map/ppermute | solution.py:20
  13.8 8.0 %collective-permute-done.refs_0_ = bf16[128,512]{1,0:T(8,128)(2,1)S(1)} collective-permute-done((bf16[128,512]{1,0:T(8,128)(2,1)}, bf16[128,512]{1,0:T(8,128)(2,1)S(1)}, u32[]{:S(2)}, u32[]{:S(2)}) %collective-permute-start) | collective-permute-done | bytes 131104 | tf_op jit(solution)/shard_map/ppermute | solution.py:20
  21.8 0.0 copy-start
  21.8 0.0 collective-permute-done.1.refs_1_
  21.8 0.0 copy-start.1
  21.8 2.2 %collective-permute-done.2.refs_3_ = bf16[128,512]{1,0:T(8,128)(2,1)S(1)} collective-permute-done((bf16[128,512]{1,0:T(8,128)(2,1)}, bf16[128,512]{1,0:T(8,128)(2,1)S(1)}, u32[]{:S(2)}, u32[]{:S(2)}) %collective-permute-start.2) | collective-permute-done | bytes 131104 | tf_op jit(solution)/shard_map/ppermute | solution.py:20
  24.0 0.0 copy-start.2
  24.0 0.0 collective-permute-done.3.refs_4_
  24.0 0.0 copy-done
  24.0 0.0 copy-done.1
  24.0 0.6 %copy-done.2 = bf16[128,512]{1,0:T(8,128)(2,1)} copy-done((bf16[128,512]{1,0:T(8,128)(2,1)}, bf16[128,512]{1,0:T(8,128)(2,1)S(1)}, u32[]{:S(2)}) %copy-start.2) | copy-done | bytes 131096
  24.6 0.0 copy-start.3
  24.6 0.6 %copy-done.3 = bf16[128,512]{1,0:T(8,128)(2,1)} copy-done((bf16[128,512]{1,0:T(8,128)(2,1)}, bf16[128,512]{1,0:T(8,128)(2,1)S(1)}, u32[]{:S(2)}) %copy-start.3) | copy-done | bytes 131096
  25.3 6.0 %attend.1 = bf16[128,4096]{1,0:T(8,128)(2,1)} custom-call(s32[32]{0:T(128)} %lengths_ref.1, bf16[128,4096]{1,0:T(8,128)(2,1)} %q_ref.1, bf16[128,512]{1,0:T(8,128)(2,1)} %copy-done, bf16[128,512]{1,0:T(8,128)(2,1)} %copy-done.1, bf16[128,512]{1,0:T(8,128)(2,1)} %refs_2_.1, bf16[128,512]{1,0:T(8,128)(2,1)} %copy-done.2, bf16[128,512]{1,0:T(8,128)(2,1)} %copy-done.3, ...), custom_call_target="tpu_custom_call" | custom-call | tf_op jit(solution)/shard_map/attend/pallas_call | solution.py:72
Async XLA Ops:
  0.0 21.8 %collective-permute-start = (bf16[128,512]{1,0:T(8,128)(2,1)}, bf16[128,512]{1,0:T(8,128)(2,1)S(1)}, u32[]{:S(2)}, u32[]{:S(2)}) collective-permute-start(bf16[128,512]{1,0:T(8,128)(2,1)} %refs_2_.1), channel_id=1, source_target_pairs={{0,2},{1,3},{2,4},{3,5},{4,6},{5,7},{6,8},{7,9},{8,10},{9,11},{10,... | collective-permute-start | bytes 393224 | tf_op jit(solution)/shard_map/ppermute | solution.py:20
  4.5 17.3 %collective-permute-start.1 = (bf16[128,512]{1,0:T(8,128)(2,1)}, bf16[128,512]{1,0:T(8,128)(2,1)S(1)}, u32[]{:S(2)}, u32[]{:S(2)}) collective-permute-start(bf16[128,512]{1,0:T(8,128)(2,1)} %refs_2_.1), channel_id=1, source_target_pairs={{0,1},{1,2},{2,3},{3,4},{4,5},{5,6},{6,7},{7,8},{8,9},{9,10},{10,1... | collective-permute-start | bytes 393224 | tf_op jit(solution)/shard_map/ppermute | solution.py:20
  8.0 16.0 %collective-permute-start.2 = (bf16[128,512]{1,0:T(8,128)(2,1)}, bf16[128,512]{1,0:T(8,128)(2,1)S(1)}, u32[]{:S(2)}, u32[]{:S(2)}) collective-permute-start(bf16[128,512]{1,0:T(8,128)(2,1)} %refs_5_.1), channel_id=1, source_target_pairs={{0,2},{1,3},{2,4},{3,5},{4,6},{5,7},{6,8},{7,9},{8,10},{9,11},{10,... | collective-permute-start | bytes 393224 | tf_op jit(solution)/shard_map/ppermute | solution.py:20
  9.9 14.0 %collective-permute-start.3 = (bf16[128,512]{1,0:T(8,128)(2,1)}, bf16[128,512]{1,0:T(8,128)(2,1)S(1)}, u32[]{:S(2)}, u32[]{:S(2)}) collective-permute-start(bf16[128,512]{1,0:T(8,128)(2,1)} %refs_5_.1), channel_id=1, source_target_pairs={{0,1},{1,2},{2,3},{3,4},{4,5},{5,6},{6,7},{7,8},{8,9},{9,10},{10,1... | collective-permute-start | bytes 393224 | tf_op jit(solution)/shard_map/ppermute | solution.py:20
  21.8 2.2 %copy-start = (bf16[128,512]{1,0:T(8,128)(2,1)}, bf16[128,512]{1,0:T(8,128)(2,1)S(1)}, u32[]{:S(2)}) copy-start(bf16[128,512]{1,0:T(8,128)(2,1)S(1)} %collective-permute-done.refs_0_) | copy-start | bytes 393220
  21.8 2.2 %copy-start.1 = (bf16[128,512]{1,0:T(8,128)(2,1)}, bf16[128,512]{1,0:T(8,128)(2,1)S(1)}, u32[]{:S(2)}) copy-start(bf16[128,512]{1,0:T(8,128)(2,1)S(1)} %collective-permute-done.1.refs_1_) | copy-start | bytes 393220
  24.0 0.7 %copy-start.2 = (bf16[128,512]{1,0:T(8,128)(2,1)}, bf16[128,512]{1,0:T(8,128)(2,1)S(1)}, u32[]{:S(2)}) copy-start(bf16[128,512]{1,0:T(8,128)(2,1)S(1)} %collective-permute-done.2.refs_3_) | copy-start | bytes 393220
  24.6 0.7 %copy-start.3 = (bf16[128,512]{1,0:T(8,128)(2,1)}, bf16[128,512]{1,0:T(8,128)(2,1)S(1)}, u32[]{:S(2)}) copy-start(bf16[128,512]{1,0:T(8,128)(2,1)S(1)} %collective-permute-done.3.refs_4_) | copy-start | bytes 393220

commit v2 on v1

v2 whole, which is shorter than its diff:
```python
import functools
import math

import jax
import jax.numpy as jnp
from jax import lax
from jax.experimental import pallas as pl
from jax.experimental.pallas import tpu as pltpu
from jax.sharding import PartitionSpec as P

HD = 128
STACK = 4
VMEM_LIMIT = 24 << 20

AXES = ("dp", "seq")
score_scale = 0.08838834764831845
neg_fill = -1e30
exp2_scale = score_scale * math.log2(math.e)

F32 = jnp.float32
BF16 = jnp.bfloat16


def shift(block, distance, keep=lambda target: True):
    count = lax.axis_size(AXES)
    return lax.ppermute(
        block, AXES, [(t - distance, t) for t in range(distance, count) if keep(t)]
    )


def head(index, count=1):
    return slice(index * HD, (index + count) * HD)


def row_stack(ref, columns):
    return jnp.concatenate([ref[:, at] for at in columns], axis=0)


def mask_bias(lengths_ref, rows, span):
    first = lax.axis_index(AXES) * rows
    key_pos = lax.broadcasted_iota(jnp.int32, (8, span), 1) + (first - span + rows)

    def step(i, carry):
        end, last = carry
        end = end + lengths_ref[i]
        return end, jnp.where(key_pos < end, jnp.minimum(last, end - 1), last)

    top = jnp.full((8, span), jnp.iinfo(jnp.int32).max, jnp.int32)
    _, last = lax.fori_loop(0, lengths_ref.shape[0], step, (jnp.int32(0), top), unroll=4)
    last = jnp.where(key_pos < 0, -1, last)
    query_pos = lax.broadcasted_iota(jnp.int32, (rows, span), 0) + first
    allowed = (query_pos >= key_pos[:1]) & (query_pos <= last[:1])
    return jnp.where(allowed, 0.0, neg_fill)


def near_kernel(chunks, group, lengths_ref, q_ref, *refs):
    key_refs = refs[:chunks]
    value_refs = refs[chunks : 2 * chunks]
    max_ref, sum_ref, mixed_ref, far_bias_ref, value_ref = refs[2 * chunks :]
    rows = q_ref.shape[0]
    span = chunks * rows
    shared = key_refs[0].shape[1] // HD
    bias = mask_bias(lengths_ref, rows, span + rows)
    far_bias_ref[...] = bias[:, :rows]
    bias = jnp.concatenate([bias[:, rows:]] * STACK, axis=0)
    value_ref[:, HD:] = jnp.ones((span, HD), value_ref.dtype)
    for kv in range(shared):
        keys = jnp.concatenate([ref[:, head(kv)] for ref in key_refs], axis=0)
        for i, ref in enumerate(value_refs):
            value_ref[i * rows : (i + 1) * rows, :HD] = ref[:, head(kv)]
        values = value_ref[...]
        for first in range(kv * group, (kv + 1) * group, STACK):
            columns = [head(first + i) for i in range(STACK)]
            scores = lax.dot_general(
                row_stack(q_ref, columns),
                keys,
                (((1,), (1,)), ((), ())),
                preferred_element_type=F32,
            )
            scores = scores + bias
            row_max = jnp.max(scores, axis=1, keepdims=True)
            weights = jnp.exp2((scores - row_max) * exp2_scale).astype(BF16)
            mixed = jnp.dot(weights, values, preferred_element_type=F32)
            row_max = jnp.broadcast_to(row_max, (STACK * rows, HD))
            for i, at in enumerate(columns):
                part = slice(i * rows, (i + 1) * rows)
                max_ref[:, at] = row_max[part]
                mixed_ref[:, at] = mixed[part, :HD]
                sum_ref[:, at] = mixed[part, HD:]


def block_diagonal(ref, a, b, scratch):
    rows = ref.shape[0]
    scratch[:rows, :HD] = ref[:, head(a)]
    scratch[rows:, HD:] = ref[:, head(b)]
    scratch[:rows, HD:] = jnp.zeros((rows, HD), scratch.dtype)
    scratch[rows:, :HD] = jnp.zeros((rows, HD), scratch.dtype)
    return scratch[...]


def far_kernel(group, q_ref, key_ref, value_ref, relay_ref, bias_ref, max_ref, sum_ref, mixed_ref, out_ref,
               far_value_ref, pair_keys, pair_values, staged_ref, sems):
    rows = q_ref.shape[0]
    shared = key_ref.shape[1] // HD
    far_value_ref[...] = value_ref[...] + relay_ref[...]
    bias = jnp.concatenate([bias_ref[...]] * STACK, axis=0)
    bias = jnp.concatenate([bias] * 2, axis=1)
    copies = []
    for a in range(0, shared, 2):
        b = a + 1
        keys = block_diagonal(key_ref, a, b, pair_keys)
        values = block_diagonal(far_value_ref, a, b, pair_values)
        for first in range(0, group, STACK):
            left = [head(a * group + first + i) for i in range(STACK)]
            right = [head(b * group + first + i) for i in range(STACK)]

            def both(ref):
                return jnp.concatenate([row_stack(ref, left), row_stack(ref, right)], axis=1)

            scores = lax.dot_general(
                both(q_ref), keys, (((1,), (1,)), ((), ())), preferred_element_type=F32
            )
            scores = scores + bias
            old_max = both(max_ref)
            far_max = jnp.concatenate(
                [
                    jnp.broadcast_to(
                        jnp.max(scores[:, head(i)], axis=1, keepdims=True), (STACK * rows, HD)
                    )
                    for i in range(2)
                ],
                axis=1,
            )
            new_max = jnp.maximum(old_max, far_max)
            weights = jnp.exp2((scores - new_max) * exp2_scale)
            fade = jnp.exp2((old_max - new_max) * exp2_scale)
            far_sum = jnp.concatenate(
                [
                    jnp.broadcast_to(
                        jnp.sum(weights[:, head(i)], axis=1, keepdims=True), (STACK * rows, HD)
                    )
                    for i in range(2)
                ],
                axis=1,
            )
            mixed = jnp.dot(weights.astype(BF16), values, preferred_element_type=F32)
            total = both(sum_ref) * fade + far_sum
            mixed = ((both(mixed_ref) * fade + mixed) / total).astype(staged_ref.dtype)
            for side, columns in enumerate((left, right)):
                for i, at in enumerate(columns):
                    staged_ref[:, at] = mixed[i * rows : (i + 1) * rows, head(side)]
                at = slice(columns[0].start, columns[-1].stop)
                copy = pltpu.make_async_copy(
                    staged_ref.at[:, at], out_ref.at[:, at], sems.at[len(copies)]
                )
                copy.start()
                copies.append(copy)
    for copy in copies:
        copy.wait()


def on_chip(array):
    return pltpu.with_memory_space_constraint(array, pltpu.VMEM)


def attend(queries, near_keys, near_values, far_keys, far_values, relayed, seq_lengths):
    rows, width = queries.shape
    chunks = len(near_keys)
    shared = far_keys.shape[1] // HD
    group = width // far_keys.shape[1]
    whole = pl.BlockSpec(memory_space=pltpu.VMEM)
    params = pltpu.CompilerParams(vmem_limit_bytes=VMEM_LIMIT)
    queries = on_chip(queries)
    state = pltpu.VMEM((rows, width), F32)
    pairs = rows * width * chunks * rows
    row_max, row_sum, mixed, far_bias = pl.pallas_call(
        functools.partial(near_kernel, chunks, group),
        in_specs=[pl.BlockSpec(memory_space=pltpu.SMEM)] + [whole] * (1 + 2 * chunks),
        out_specs=[whole] * 4,
        out_shape=[state, state, state, pltpu.VMEM((rows, rows), F32)],
        scratch_shapes=[pltpu.VMEM((chunks * rows, 2 * HD), BF16)],
        compiler_params=params,
        cost_estimate=pl.CostEstimate(
            flops=6 * pairs, transcendentals=pairs // HD, bytes_accessed=rows * width * 14
        ),
        name="near",
    )(seq_lengths, queries, *map(on_chip, near_keys), *map(on_chip, near_values))
    copies = 2 * (shared // 2) * (group // STACK)
    return pl.pallas_call(
        functools.partial(far_kernel, group),
        in_specs=[whole] * 8,
        out_specs=pl.BlockSpec(memory_space=pl.ANY),
        out_shape=jax.ShapeDtypeStruct((rows, width), queries.dtype),
        scratch_shapes=[
            pltpu.VMEM(far_keys.shape, BF16),
            pltpu.VMEM((2 * rows, 2 * HD), BF16),
            pltpu.VMEM((2 * rows, 2 * HD), BF16),
            pltpu.VMEM((rows, width), queries.dtype),
            pltpu.SemaphoreType.DMA((copies,)),
        ],
        compiler_params=params,
        name="far",
    )(queries, on_chip(far_keys), on_chip(far_values), on_chip(relayed), far_bias, row_max, row_sum, mixed)


def body(queries, key_proj, value_proj, seq_lengths):
    rows = queries.shape[0]
    reach = rows * lax.axis_size("seq") // 2
    behind = -(-reach // rows)
    near_keys, near_values = [key_proj], [value_proj]
    for distance in range(1, behind):
        near_keys.insert(0, shift(key_proj, distance))
        near_values.insert(0, shift(value_proj, distance))
    far_keys = shift(key_proj, behind)
    far_values = shift(value_proj, behind, lambda target: target % 2 == 0)
    relayed = shift(near_values[0], 1, lambda target: target % 2 == 1 and target >= behind)
    return attend(queries, near_keys, near_values, far_keys, far_values, relayed, seq_lengths)


def solution(mesh):
    return jax.shard_map(
        body,
        mesh=mesh,
        in_specs=(P(AXES, None), P(AXES, None), P(AXES, None), P()),
        out_specs=P(AXES, None),
        check_vma=False,
    )
```

time: 31.5 us -> 25.7 us (0.82)
  the two profiles are of different devices: /device:TPU:4 before, /device:TPU:1 now
where the time goes in v2:
time: 25.7 us; the launch traced here: 25.4 us
  starting transfers between devices  16.7 us (65%)
  Pallas kernels  4.92 us (19%)
  local copies, waits for them, and re-layouts  3.68 us (14%)
    ppermute x5, starting transfers between devices, shift(): lax.ppermute(block, AXES, [(t - distance, t) for t in range(distance, cou...  16.7 us
    unnamed x8, local copies, waits for them, and re-layouts  3.68 us
    pallas_call x1, Pallas kernels, attend(): pl.pallas_call(functools.partial(far_kernel, group), in_specs=[whole] * 8...  2.75 us
    pallas_call x1, Pallas kernels, attend(): pl.pallas_call(functools.partial(near_kernel, chunks, group), in_specs=[p...  2.17 us
  transfers between devices with their start and end apart: 5, of which 0 were waited for; matrix products, arithmetic and copies ran while one was open for 0% of the time, Pallas kernels for 9%

profile of v2, /device:TPU:1, one launch (start us, length us, event | category | flops | bytes accessed | tf_op | source)
XLA Modules:
  0.0 25.4 jit_solution(17159647788491789137)
XLA Ops:
  0.0 4.0 %collective-permute-start.2 = (bf16[128,512]{1,0:T(8,128)(2,1)}, bf16[128,512]{1,0:T(8,128)(2,1)S(1)}, u32[]{:S(2)}, u32[]{:S(2)}) collective-permute-start(bf16[128,512]{1,0:T(8,128)(2,1)} %refs_3_.1), channel_id=1, source_target_pairs={{0,1},{1,2},{2,3},{3,4},{4,5},{5,6},{6,7},{7,8},{8,9},{9,10},{10,1... | collective-permute-start | bytes 393224 | tf_op jit(solution)/shard_map/ppermute | solution.py:26
  4.0 3.2 %collective-permute-start.4 = (bf16[128,512]{1,0:T(8,128)(2,1)}, bf16[128,512]{1,0:T(8,128)(2,1)S(1)}, u32[]{:S(2)}, u32[]{:S(2)}) collective-permute-start(bf16[128,512]{1,0:T(8,128)(2,1)} %refs_1_.1), channel_id=1, source_target_pairs={{0,1},{1,2},{2,3},{3,4},{4,5},{5,6},{6,7},{7,8},{8,9},{9,10},{10,1... | collective-permute-start | bytes 393224 | tf_op jit(solution)/shard_map/ppermute | solution.py:26
  7.2 4.4 %collective-permute-start = (bf16[128,512]{1,0:T(8,128)(2,1)}, bf16[128,512]{1,0:T(8,128)(2,1)S(1)}, u32[]{:S(2)}, u32[]{:S(2)}) collective-permute-start(bf16[128,512]{1,0:T(8,128)(2,1)} %refs_1_.1), channel_id=1, source_target_pairs={{0,2},{1,3},{2,4},{3,5},{4,6},{5,7},{6,8},{7,9},{8,10},{9,11},{10,... | collective-permute-start | bytes 393224 | tf_op jit(solution)/shard_map/ppermute | solution.py:26
  11.6 3.9 %collective-permute-start.1 = (bf16[128,512]{1,0:T(8,128)(2,1)}, bf16[128,512]{1,0:T(8,128)(2,1)S(1)}, u32[]{:S(2)}, u32[]{:S(2)}) collective-permute-start(bf16[128,512]{1,0:T(8,128)(2,1)} %refs_3_.1), channel_id=1, source_target_pairs={{0,2},{2,4},{4,6},{6,8},{8,10},{10,12},{12,14},{14,16},{16,18},{18... | collective-permute-start | bytes 393224 | tf_op jit(solution)/shard_map/ppermute | solution.py:26
  15.5 0.0 collective-permute-done.2.refs_2_
  15.5 1.3 %collective-permute-start.3 = (bf16[128,512]{1,0:T(8,128)(2,1)S(1)}, bf16[128,512]{1,0:T(8,128)(2,1)S(1)}, u32[]{:S(2)}, u32[]{:S(2)}) collective-permute-start(bf16[128,512]{1,0:T(8,128)(2,1)S(1)} %collective-permute-done.2.refs_2_), channel_id=1, source_target_pairs={{2,3},{4,5},{6,7},{8,9},{10,11},{12,13},{14,15},{16,17},{18,19},{2... | collective-permute-start | bytes 393224 | tf_op jit(solution)/shard_map/ppermute | solution.py:26
  16.8 0.0 collective-permute-done.4.refs_0_
  16.8 0.0 copy-start
  16.8 1.2 %copy-done = bf16[128,4096]{1,0:T(8,128)(2,1)S(1)} copy-done((bf16[128,4096]{1,0:T(8,128)(2,1)S(1)}, bf16[128,4096]{1,0:T(8,128)(2,1)}, u32[]{:S(2)}) %copy-start) | copy-done | bytes 1048600
  18.0 0.0 copy-start.1
  18.0 0.9 %copy-done.1 = bf16[128,512]{1,0:T(8,128)(2,1)S(1)} copy-done((bf16[128,512]{1,0:T(8,128)(2,1)S(1)}, bf16[128,512]{1,0:T(8,128)(2,1)}, u32[]{:S(2)}) %copy-start.1) | copy-done | bytes 131096
  18.9 0.0 copy-start.2
  18.9 0.9 %copy-done.2 = bf16[128,512]{1,0:T(8,128)(2,1)S(1)} copy-done((bf16[128,512]{1,0:T(8,128)(2,1)S(1)}, bf16[128,512]{1,0:T(8,128)(2,1)}, u32[]{:S(2)}) %copy-start.2) | copy-done | bytes 131096
  19.8 0.0 copy-start.3
  19.8 0.7 %copy-done.3 = s32[32]{0:T(128)S(1)} copy-done((s32[32]{0:T(128)S(1)}, s32[32]{0:T(128)}, u32[]{:S(2)}) %copy-start.3) | copy-done | bytes 152
  20.5 2.2 %near.1 = (f32[128,4096]{1,0:T(8,128)S(1)}, f32[128,4096]{1,0:T(8,128)S(1)}, f32[128,4096]{1,0:T(8,128)S(1)}, f32[128,128]{1,0:T(8,128)S(1)}) custom-call(s32[32]{0:T(128)S(1)} %copy-done.3, bf16[128,4096]{1,0:T(8,128)(2,1)S(1)} %copy-done, bf16[128,512]{1,0:T(8,128)(2,1)S(1)} %collective-permute-done.4.refs_0_, bf16[128,512]{1,0:T(8,128)(2,1)S(1)} %copy-done.1, ...), custom_call_target="tpu_custom_call" | custom-call | flops 805306368 | bytes 7340032 | tf_op jit(solution)/shard_map/near/pallas_call | solution.py:176
  22.7 0.0 collective-permute-done.key_ref
  22.7 0.0 collective-permute-done.1.value_ref
  22.7 0.0 collective-permute-done.3.relay_ref
  22.7 2.8 %far.1 = bf16[128,4096]{1,0:T(8,128)(2,1)} custom-call(bf16[128,4096]{1,0:T(8,128)(2,1)S(1)} %copy-done, bf16[128,512]{1,0:T(8,128)(2,1)S(1)} %collective-permute-done.key_ref, bf16[128,512]{1,0:T(8,128)(2,1)S(1)} %collective-permute-done.1.value_ref, bf16[128,512]{1,0:T(8,128)(2,1)S(1)} %collective-permute-done.3.relay_ref, ...), custom_call_target="tpu_custom_call" | custom-call | tf_op jit(solution)/shard_map/far/pallas_call | solution.py:189
Async XLA Ops:
  0.0 15.5 %collective-permute-start.2 = (bf16[128,512]{1,0:T(8,128)(2,1)}, bf16[128,512]{1,0:T(8,128)(2,1)S(1)}, u32[]{:S(2)}, u32[]{:S(2)}) collective-permute-start(bf16[128,512]{1,0:T(8,128)(2,1)} %refs_3_.1), channel_id=1, source_target_pairs={{0,1},{1,2},{2,3},{3,4},{4,5},{5,6},{6,7},{7,8},{8,9},{9,10},{10,1... | collective-permute-start | bytes 393224 | tf_op jit(solution)/shard_map/ppermute | solution.py:26
  4.0 12.8 %collective-permute-start.4 = (bf16[128,512]{1,0:T(8,128)(2,1)}, bf16[128,512]{1,0:T(8,128)(2,1)S(1)}, u32[]{:S(2)}, u32[]{:S(2)}) collective-permute-start(bf16[128,512]{1,0:T(8,128)(2,1)} %refs_1_.1), channel_id=1, source_target_pairs={{0,1},{1,2},{2,3},{3,4},{4,5},{5,6},{6,7},{7,8},{8,9},{9,10},{10,1... | collective-permute-start | bytes 393224 | tf_op jit(solution)/shard_map/ppermute | solution.py:26
  7.2 15.4 %collective-permute-start = (bf16[128,512]{1,0:T(8,128)(2,1)}, bf16[128,512]{1,0:T(8,128)(2,1)S(1)}, u32[]{:S(2)}, u32[]{:S(2)}) collective-permute-start(bf16[128,512]{1,0:T(8,128)(2,1)} %refs_1_.1), channel_id=1, source_target_pairs={{0,2},{1,3},{2,4},{3,5},{4,6},{5,7},{6,8},{7,9},{8,10},{9,11},{10,... | collective-permute-start | bytes 393224 | tf_op jit(solution)/shard_map/ppermute | solution.py:26
  11.6 11.1 %collective-permute-start.1 = (bf16[128,512]{1,0:T(8,128)(2,1)}, bf16[128,512]{1,0:T(8,128)(2,1)S(1)}, u32[]{:S(2)}, u32[]{:S(2)}) collective-permute-start(bf16[128,512]{1,0:T(8,128)(2,1)} %refs_3_.1), channel_id=1, source_target_pairs={{0,2},{2,4},{4,6},{6,8},{8,10},{10,12},{12,14},{14,16},{16,18},{18... | collective-permute-start | bytes 393224 | tf_op jit(solution)/shard_map/ppermute | solution.py:26
  15.5 7.2 %collective-permute-start.3 = (bf16[128,512]{1,0:T(8,128)(2,1)S(1)}, bf16[128,512]{1,0:T(8,128)(2,1)S(1)}, u32[]{:S(2)}, u32[]{:S(2)}) collective-permute-start(bf16[128,512]{1,0:T(8,128)(2,1)S(1)} %collective-permute-done.2.refs_2_), channel_id=1, source_target_pairs={{2,3},{4,5},{6,7},{8,9},{10,11},{12,13},{14,15},{16,17},{18,19},{2... | collective-permute-start | bytes 393224 | tf_op jit(solution)/shard_map/ppermute | solution.py:26
  16.8 1.2 %copy-start = (bf16[128,4096]{1,0:T(8,128)(2,1)S(1)}, bf16[128,4096]{1,0:T(8,128)(2,1)}, u32[]{:S(2)}) copy-start(bf16[128,4096]{1,0:T(8,128)(2,1)} %q_ref.3) | copy-start | bytes 3145732
  18.0 0.9 %copy-start.1 = (bf16[128,512]{1,0:T(8,128)(2,1)S(1)}, bf16[128,512]{1,0:T(8,128)(2,1)}, u32[]{:S(2)}) copy-start(bf16[128,512]{1,0:T(8,128)(2,1)} %refs_1_.1) | copy-start | bytes 393220
  18.9 0.9 %copy-start.2 = (bf16[128,512]{1,0:T(8,128)(2,1)S(1)}, bf16[128,512]{1,0:T(8,128)(2,1)}, u32[]{:S(2)}) copy-start(bf16[128,512]{1,0:T(8,128)(2,1)} %refs_3_.1) | copy-start | bytes 393220
  19.8 0.7 %copy-start.3 = (s32[32]{0:T(128)S(1)}, s32[32]{0:T(128)}, u32[]{:S(2)}) copy-start(s32[32]{0:T(128)} %lengths_ref.1) | copy-start | bytes 388

commit v3 on v2

v3 whole, which is shorter than its diff:
```python
import functools
import math

import jax
import jax.numpy as jnp
from jax import lax
from jax.experimental import pallas as pl
from jax.experimental.pallas import tpu as pltpu
from jax.sharding import PartitionSpec as P

HD = 128
STACK = 4
VMEM_LIMIT = 24 << 20

AXES = ("dp", "seq")
score_scale = 0.08838834764831845
neg_fill = -1e30
exp2_scale = score_scale * math.log2(math.e)

F32 = jnp.float32
BF16 = jnp.bfloat16


def shift(block, distance, keep=lambda target: True):
    count = lax.axis_size(AXES)
    return lax.ppermute(
        block, AXES, [(t - distance, t) for t in range(distance, count) if keep(t)]
    )


def head(index, count=1):
    return slice(index * HD, (index + count) * HD)


def row_stack(ref, columns):
    return jnp.concatenate([ref[:, at] for at in columns], axis=0)


def mask_bias(lengths_ref, rows, span):
    first = lax.axis_index(AXES) * rows
    key_pos = lax.broadcasted_iota(jnp.int32, (8, span), 1) + (first - span + rows)

    def step(i, carry):
        end, last = carry
        end = end + lengths_ref[i]
        return end, jnp.where(key_pos < end, jnp.minimum(last, end - 1), last)

    top = jnp.full((8, span), jnp.iinfo(jnp.int32).max, jnp.int32)
    _, last = lax.fori_loop(0, lengths_ref.shape[0], step, (jnp.int32(0), top), unroll=4)
    last = jnp.where(key_pos < 0, -1, last)
    query_pos = lax.broadcasted_iota(jnp.int32, (rows, span), 0) + first
    allowed = (query_pos >= key_pos[:1]) & (query_pos <= last[:1])
    return jnp.where(allowed, 0.0, neg_fill)


def near_kernel(chunks, group, lengths_ref, q_hbm, key_hbm, value_hbm, *refs):
    key_refs = refs[: chunks - 1]
    value_refs = refs[chunks - 1 : 2 * chunks - 2]
    q_ref, max_ref, sum_ref, mixed_ref, far_bias_ref, own_key, own_value, value_ref, sems = refs[
        2 * chunks - 2 :
    ]
    rows = q_ref.shape[0]
    span = chunks * rows
    shared = own_key.shape[1] // HD
    loads = [
        pltpu.make_async_copy(key_hbm, own_key, sems.at[0]),
        pltpu.make_async_copy(value_hbm, own_value, sems.at[1]),
    ]
    for kv in range(shared):
        at = head(kv * group, group)
        loads.append(pltpu.make_async_copy(q_hbm.at[:, at], q_ref.at[:, at], sems.at[2 + kv]))
    for load in loads:
        load.start()
    bias = mask_bias(lengths_ref, rows, span + rows)
    far_bias_ref[...] = bias[:, :rows]
    bias = jnp.concatenate([bias[:, rows:]] * STACK, axis=0)
    value_ref[:, HD:] = jnp.ones((span, HD), value_ref.dtype)
    loads[0].wait()
    loads[1].wait()
    for kv in range(shared):
        keys = jnp.concatenate([ref[:, head(kv)] for ref in (*key_refs, own_key)], axis=0)
        for i, ref in enumerate((*value_refs, own_value)):
            value_ref[i * rows : (i + 1) * rows, :HD] = ref[:, head(kv)]
        values = value_ref[...]
        loads[2 + kv].wait()
        for first in range(kv * group, (kv + 1) * group, STACK):
            columns = [head(first + i) for i in range(STACK)]
            scores = lax.dot_general(
                row_stack(q_ref, columns),
                keys,
                (((1,), (1,)), ((), ())),
                preferred_element_type=F32,
            )
            scores = scores + bias
            row_max = jnp.max(scores, axis=1, keepdims=True)
            weights = jnp.exp2((scores - row_max) * exp2_scale).astype(BF16)
            mixed = jnp.dot(weights, values, preferred_element_type=F32)
            row_max = jnp.broadcast_to(row_max, (STACK * rows, HD))
            for i, at in enumerate(columns):
                part = slice(i * rows, (i + 1) * rows)
                max_ref[:, at] = row_max[part]
                mixed_ref[:, at] = mixed[part, :HD]
                sum_ref[:, at] = mixed[part, HD:]


def block_diagonal(first, second, scratch):
    rows = first.shape[0]
    scratch[:rows, :HD] = first
    scratch[rows:, HD:] = second
    scratch[:rows, HD:] = jnp.zeros((rows, HD), scratch.dtype)
    scratch[rows:, :HD] = jnp.zeros((rows, HD), scratch.dtype)
    return scratch[...]


def head_pairs(shared, group):
    for a in range(0, shared, 2):
        for first in range(0, group, STACK):
            yield a, [
                [head((a + side) * group + first + i) for i in range(STACK)] for side in range(2)
            ]


def side_by_side(ref, columns):
    return jnp.concatenate([row_stack(ref, side) for side in columns], axis=1)


def put_pair(ref, columns, block):
    rows = ref.shape[0]
    for side in range(2):
        for i, at in enumerate(columns[side]):
            ref[:, at] = block[i * rows : (i + 1) * rows, head(side)]


def per_side(reduce, block):
    parts = [reduce(block[:, head(side)], axis=1, keepdims=True) for side in range(2)]
    return jnp.concatenate([jnp.broadcast_to(p, (block.shape[0], HD)) for p in parts], axis=1)


def far_kernel(group, q_ref, key_ref, bias_ref, max_ref, sum_ref, mixed_ref, weight_ref, scale_ref, faded_ref, pair_ref):
    shared = key_ref.shape[1] // HD
    bias = jnp.concatenate([bias_ref[...]] * STACK, axis=0)
    bias = jnp.concatenate([bias] * 2, axis=1)
    done = None
    for a, columns in head_pairs(shared, group):
        if a != done:
            keys = block_diagonal(key_ref[:, head(a)], key_ref[:, head(a + 1)], pair_ref)
            done = a
        scores = lax.dot_general(
            side_by_side(q_ref, columns), keys, (((1,), (1,)), ((), ())), preferred_element_type=F32
        )
        scores = scores + bias
        old_max = side_by_side(max_ref, columns)
        new_max = jnp.maximum(old_max, per_side(jnp.max, scores))
        weights = jnp.exp2((scores - new_max) * exp2_scale)
        fade = jnp.exp2((old_max - new_max) * exp2_scale)
        scale = 1.0 / (side_by_side(sum_ref, columns) * fade + per_side(jnp.sum, weights))
        put_pair(weight_ref, columns, weights.astype(BF16))
        put_pair(scale_ref, columns, scale)
        put_pair(faded_ref, columns, side_by_side(mixed_ref, columns) * (fade * scale))


def last_kernel(group, value_ref, relay_ref, weight_ref, scale_ref, faded_ref, out_ref, pair_ref, staged_ref, sems):
    shared = value_ref.shape[1] // HD
    copies = []
    done = None
    for a, columns in head_pairs(shared, group):
        if a != done:
            values = block_diagonal(
                *[value_ref[:, head(kv)] + relay_ref[:, head(kv)] for kv in (a, a + 1)], pair_ref
            )
            done = a
        mixed = jnp.dot(side_by_side(weight_ref, columns), values, preferred_element_type=F32)
        mixed = side_by_side(faded_ref, columns) + mixed * side_by_side(scale_ref, columns)
        put_pair(staged_ref, columns, mixed.astype(staged_ref.dtype))
        for side in columns:
            at = slice(side[0].start, side[-1].stop)
            copies.append(
                pltpu.make_async_copy(
                    staged_ref.at[:, at], out_ref.at[:, at], sems.at[len(copies)]
                )
            )
            copies[-1].start()
    for copy in copies:
        copy.wait()


def on_chip(array):
    return pltpu.with_memory_space_constraint(array, pltpu.VMEM)


def off_chip(array):
    return pltpu.with_memory_space_constraint(array, pltpu.HBM)


def attend(queries, near_keys, near_values, far_keys, far_values, relayed, seq_lengths):
    rows, width = queries.shape
    chunks = len(near_keys)
    shared = far_keys.shape[1] // HD
    group = width // far_keys.shape[1]
    whole = pl.BlockSpec(memory_space=pltpu.VMEM)
    outside = pl.BlockSpec(memory_space=pltpu.HBM)
    params = pltpu.CompilerParams(vmem_limit_bytes=VMEM_LIMIT)
    wide = pltpu.VMEM((rows, width), F32)
    narrow = pltpu.VMEM((rows, width), BF16)
    own = pltpu.VMEM(far_keys.shape, BF16)
    pair = pltpu.VMEM((2 * rows, 2 * HD), BF16)
    pairs = rows * width * rows
    *near_keys, own_keys = near_keys
    *near_values, own_values = near_values
    queries, row_max, row_sum, mixed, far_bias = pl.pallas_call(
        functools.partial(near_kernel, chunks, group),
        in_specs=[pl.BlockSpec(memory_space=pltpu.SMEM)] + [outside] * 3 + [whole] * (2 * chunks - 2),
        out_specs=[whole] * 5,
        out_shape=[narrow, wide, wide, wide, pltpu.VMEM((rows, rows), F32)],
        scratch_shapes=[
            own,
            own,
            pltpu.VMEM((chunks * rows, 2 * HD), BF16),
            pltpu.SemaphoreType.DMA((2 + shared,)),
        ],
        compiler_params=params,
        cost_estimate=pl.CostEstimate(
            flops=6 * chunks * pairs, transcendentals=chunks * pairs // HD, bytes_accessed=rows * width * 14
        ),
        name="near",
    )(
        *map(off_chip, (seq_lengths, queries, own_keys, own_values)),
        *map(on_chip, near_keys),
        *map(on_chip, near_values),
    )
    weights, scale, faded = pl.pallas_call(
        functools.partial(far_kernel, group),
        in_specs=[whole] * 6,
        out_specs=[whole] * 3,
        out_shape=[narrow, wide, wide],
        scratch_shapes=[pair],
        compiler_params=params,
        cost_estimate=pl.CostEstimate(
            flops=2 * pairs, transcendentals=pairs // HD, bytes_accessed=rows * width * 24
        ),
        name="far",
    )(queries, on_chip(far_keys), far_bias, row_max, row_sum, mixed)
    copies = 2 * (shared // 2) * (group // STACK)
    return pl.pallas_call(
        functools.partial(last_kernel, group),
        in_specs=[whole] * 5,
        out_specs=outside,
        out_shape=jax.ShapeDtypeStruct((rows, width), queries.dtype),
        scratch_shapes=[pair, narrow, pltpu.SemaphoreType.DMA((copies,))],
        compiler_params=params,
        name="last",
    )(on_chip(far_values), on_chip(relayed), weights, scale, faded)


def body(queries, key_proj, value_proj, seq_lengths):
    rows = queries.shape[0]
    reach = rows * lax.axis_size("seq") // 2
    behind = -(-reach // rows)
    near_keys, near_values = [key_proj], [value_proj]
    for distance in range(1, behind):
        near_keys.insert(0, shift(key_proj, distance))
        near_values.insert(0, shift(value_proj, distance))
    far_keys = shift(key_proj, behind)
    far_values = shift(value_proj, behind, lambda target: target % 2 == 0)
    relayed = shift(near_values[0], 1, lambda target: target % 2 == 1 and target >= behind)
    return attend(queries, near_keys, near_values, far_keys, far_values, relayed, seq_lengths)


def solution(mesh):
    return jax.shard_map(
        body,
        mesh=mesh,
        in_specs=(P(AXES, None), P(AXES, None), P(AXES, None), P()),
        out_specs=P(AXES, None),
        check_vma=False,
    )
```

time: 25.7 us -> 24.8 us (0.965)
  local copies, waits for them, and re-layouts: 3.68 us -> 0 us
  Pallas kernels: 4.92 us -> 7.74 us
    unnamed x8 -> x0, local copies, waits for them, and re-layouts: 3.68 us -> none
    pallas_call x1, Pallas kernels: 2.17 us -> 4.31 us  [attend(): pl.pallas_call(functools.partial(near_kernel, chunks, group), in_specs=[p...]
    pallas_call x1 -> x2, Pallas kernels: 2.75 us -> 3.42 us  [the longest x1 1.83 us: attend(): pl.pallas_call(functools.partial(far_kernel, group), in_specs=[whole] * 6...]
  transfers between devices with their start and end apart: 5 -> 5, of which waited for: 0 -> 0; matrix products, arithmetic and copies ran while one was open for 0% -> 0% of each run, Pallas kernels for 9% -> 25%
where the time goes in v3:
time: 24.8 us; the launch traced here: 24.6 us
  starting transfers between devices  16.7 us (67%)
  Pallas kernels  7.74 us (31%)
    ppermute x5, starting transfers between devices, shift(): lax.ppermute(block, AXES, [(t - distance, t) for t in range(distance, cou...  16.7 us
    pallas_call x1, Pallas kernels, attend(): pl.pallas_call(functools.partial(near_kernel, chunks, group), in_specs=[p...  4.31 us
    pallas_call x1, Pallas kernels, attend(): pl.pallas_call(functools.partial(far_kernel, group), in_specs=[whole] * 6...  1.83 us
    pallas_call x1, Pallas kernels, attend(): pl.pallas_call(functools.partial(last_kernel, group), in_specs=[whole] *...  1.59 us
  transfers between devices with their start and end apart: 5, of which 0 were waited for; matrix products, arithmetic and copies ran while one was open for 0% of the time, Pallas kernels for 25%

profile of v3, /device:TPU:1, one launch (start us, length us, event | category | flops | bytes accessed | tf_op | source)
XLA Modules:
  0.0 24.6 jit_solution(4615526851416774412)
XLA Ops:
  0.0 4.0 %collective-permute-start.1 = (bf16[128,512]{1,0:T(8,128)(2,1)}, bf16[128,512]{1,0:T(8,128)(2,1)S(1)}, u32[]{:S(2)}, u32[]{:S(2)}) collective-permute-start(bf16[128,512]{1,0:T(8,128)(2,1)} %value_hbm.1), channel_id=1, source_target_pairs={{0,1},{1,2},{2,3},{3,4},{4,5},{5,6},{6,7},{7,8},{8,9},{9,10},{10,1... | collective-permute-start | bytes 393224 | tf_op jit(solution)/shard_map/ppermute | solution.py:26
  4.0 3.2 %collective-permute-start.3 = (bf16[128,512]{1,0:T(8,128)(2,1)}, bf16[128,512]{1,0:T(8,128)(2,1)S(1)}, u32[]{:S(2)}, u32[]{:S(2)}) collective-permute-start(bf16[128,512]{1,0:T(8,128)(2,1)} %key_hbm.1), channel_id=1, source_target_pairs={{0,1},{1,2},{2,3},{3,4},{4,5},{5,6},{6,7},{7,8},{8,9},{9,10},{10,1... | collective-permute-start | bytes 393224 | tf_op jit(solution)/shard_map/ppermute | solution.py:26
  7.2 4.4 %collective-permute-start.4 = (bf16[128,512]{1,0:T(8,128)(2,1)}, bf16[128,512]{1,0:T(8,128)(2,1)S(1)}, u32[]{:S(2)}, u32[]{:S(2)}) collective-permute-start(bf16[128,512]{1,0:T(8,128)(2,1)} %key_hbm.1), channel_id=1, source_target_pairs={{0,2},{1,3},{2,4},{3,5},{4,6},{5,7},{6,8},{7,9},{8,10},{9,11},{10,... | collective-permute-start | bytes 393224 | tf_op jit(solution)/shard_map/ppermute | solution.py:26
  11.6 3.9 %collective-permute-start = (bf16[128,512]{1,0:T(8,128)(2,1)}, bf16[128,512]{1,0:T(8,128)(2,1)S(1)}, u32[]{:S(2)}, u32[]{:S(2)}) collective-permute-start(bf16[128,512]{1,0:T(8,128)(2,1)} %value_hbm.1), channel_id=1, source_target_pairs={{0,2},{2,4},{4,6},{6,8},{8,10},{10,12},{12,14},{14,16},{16,18},{18... | collective-permute-start | bytes 393224 | tf_op jit(solution)/shard_map/ppermute | solution.py:26
  15.5 0.0 collective-permute-done.1.refs_1_
  15.5 1.3 %collective-permute-start.2 = (bf16[128,512]{1,0:T(8,128)(2,1)S(1)}, bf16[128,512]{1,0:T(8,128)(2,1)S(1)}, u32[]{:S(2)}, u32[]{:S(2)}) collective-permute-start(bf16[128,512]{1,0:T(8,128)(2,1)S(1)} %collective-permute-done.1.refs_1_), channel_id=1, source_target_pairs={{2,3},{4,5},{6,7},{8,9},{10,11},{12,13},{14,15},{16,17},{18,19},{2... | collective-permute-start | bytes 393224 | tf_op jit(solution)/shard_map/ppermute | solution.py:26
  16.8 0.0 collective-permute-done.3.refs_0_
  16.8 4.3 %near.1 = (bf16[128,4096]{1,0:T(8,128)(2,1)S(1)}, f32[128,4096]{1,0:T(8,128)S(1)}, f32[128,4096]{1,0:T(8,128)S(1)}, f32[128,4096]{1,0:T(8,128)S(1)}, f32[128,128]{1,0:T(8,128)S(1)}) custom-call(s32[32]{0:T(128)} %lengths_ref.1, bf16[128,4096]{1,0:T(8,128)(2,1)} %q_hbm.1, bf16[128,512]{1,0:T(8,128)(2,1)} %key_hbm.1, bf16[128,512]{1,0:T(8,128)(2,1)} %value_hbm.1, ...), custom_call_target="tpu_custom_call" | custom-call | flops 805306368 | bytes 7340032 | tf_op jit(solution)/shard_map/near/pallas_call | solution.py:210
  21.1 0.0 collective-permute-done.4.key_ref
  21.1 1.8 %far.1 = (bf16[128,4096]{1,0:T(8,128)(2,1)S(1)}, f32[128,4096]{1,0:T(8,128)S(1)}, f32[128,4096]{1,0:T(8,128)S(1)}) custom-call(bf16[128,4096]{1,0:T(8,128)(2,1)S(1)} %get-tuple-element.13.q_ref, bf16[128,512]{1,0:T(8,128)(2,1)S(1)} %collective-permute-done.4.key_ref, f32[128,128]{1,0:T(8,128)S(1)} %get-tuple-element.14.bias_ref, ...), custom_call_target="tpu_custom_call" | custom-call | flops 134217728 | bytes 12582912 | tf_op jit(solution)/shard_map/far/pallas_call | solution.py:231
  23.0 0.0 collective-permute-done.value_ref
  23.0 0.0 collective-permute-done.2.relay_ref
  23.0 1.6 %last.1 = bf16[128,4096]{1,0:T(8,128)(2,1)} custom-call(bf16[128,512]{1,0:T(8,128)(2,1)S(1)} %collective-permute-done.value_ref, bf16[128,512]{1,0:T(8,128)(2,1)S(1)} %collective-permute-done.2.relay_ref, bf16[128,4096]{1,0:T(8,128)(2,1)S(1)} %get-tuple-element.18.weight_ref, f32[128,4096]{1,0:T(8,128)S(1)} %get-tuple-element.19.scale_ref, ...), custom_call_target="tpu_custom_call" | custom-call | tf_op jit(solution)/shard_map/last/pallas_call | solution.py:244
Async XLA Ops:
  0.0 15.5 %collective-permute-start.1 = (bf16[128,512]{1,0:T(8,128)(2,1)}, bf16[128,512]{1,0:T(8,128)(2,1)S(1)}, u32[]{:S(2)}, u32[]{:S(2)}) collective-permute-start(bf16[128,512]{1,0:T(8,128)(2,1)} %value_hbm.1), channel_id=1, source_target_pairs={{0,1},{1,2},{2,3},{3,4},{4,5},{5,6},{6,7},{7,8},{8,9},{9,10},{10,1... | collective-permute-start | bytes 393224 | tf_op jit(solution)/shard_map/ppermute | solution.py:26
  4.0 12.8 %collective-permute-start.3 = (bf16[128,512]{1,0:T(8,128)(2,1)}, bf16[128,512]{1,0:T(8,128)(2,1)S(1)}, u32[]{:S(2)}, u32[]{:S(2)}) collective-permute-start(bf16[128,512]{1,0:T(8,128)(2,1)} %key_hbm.1), channel_id=1, source_target_pairs={{0,1},{1,2},{2,3},{3,4},{4,5},{5,6},{6,7},{7,8},{8,9},{9,10},{10,1... | collective-permute-start | bytes 393224 | tf_op jit(solution)/shard_map/ppermute | solution.py:26
  7.2 13.9 %collective-permute-start.4 = (bf16[128,512]{1,0:T(8,128)(2,1)}, bf16[128,512]{1,0:T(8,128)(2,1)S(1)}, u32[]{:S(2)}, u32[]{:S(2)}) collective-permute-start(bf16[128,512]{1,0:T(8,128)(2,1)} %key_hbm.1), channel_id=1, source_target_pairs={{0,2},{1,3},{2,4},{3,5},{4,6},{5,7},{6,8},{7,9},{8,10},{9,11},{10,... | collective-permute-start | bytes 393224 | tf_op jit(solution)/shard_map/ppermute | solution.py:26
  11.6 11.4 %collective-permute-start = (bf16[128,512]{1,0:T(8,128)(2,1)}, bf16[128,512]{1,0:T(8,128)(2,1)S(1)}, u32[]{:S(2)}, u32[]{:S(2)}) collective-permute-start(bf16[128,512]{1,0:T(8,128)(2,1)} %value_hbm.1), channel_id=1, source_target_pairs={{0,2},{2,4},{4,6},{6,8},{8,10},{10,12},{12,14},{14,16},{16,18},{18... | collective-permute-start | bytes 393224 | tf_op jit(solution)/shard_map/ppermute | solution.py:26
  15.5 7.5 %collective-permute-start.2 = (bf16[128,512]{1,0:T(8,128)(2,1)S(1)}, bf16[128,512]{1,0:T(8,128)(2,1)S(1)}, u32[]{:S(2)}, u32[]{:S(2)}) collective-permute-start(bf16[128,512]{1,0:T(8,128)(2,1)S(1)} %collective-permute-done.1.refs_1_), channel_id=1, source_target_pairs={{2,3},{4,5},{6,7},{8,9},{10,11},{12,13},{14,15},{16,17},{18,19},{2... | collective-permute-start | bytes 393224 | tf_op jit(solution)/shard_map/ppermute | solution.py:26

commit v4 on v3

--- a/solution.py
+++ b/solution.py
@@ -9,7 +9,10 @@
 from jax.sharding import PartitionSpec as P
 
 HD = 128
-STACK = 4
+NEAR_STACK = 2
+FAR_STACK = 2
+LAST_STACK = 2
+PIECE = 4
 VMEM_LIMIT = 24 << 20
 
 AXES = ("dp", "seq")
@@ -53,38 +56,49 @@
     return jnp.where(allowed, 0.0, neg_fill)
 
 
-def near_kernel(chunks, group, lengths_ref, q_hbm, key_hbm, value_hbm, *refs):
+def near_kernel(chunks, group, lengths_hbm, q_hbm, key_hbm, value_hbm, *refs):
     key_refs = refs[: chunks - 1]
     value_refs = refs[chunks - 1 : 2 * chunks - 2]
-    q_ref, max_ref, sum_ref, mixed_ref, far_bias_ref, own_key, own_value, value_ref, sems = refs[
-        2 * chunks - 2 :
-    ]
+    (
+        q_ref,
+        max_ref,
+        sum_ref,
+        mixed_ref,
+        far_bias_ref,
+        lengths_ref,
+        own_key,
+        own_value,
+        value_ref,
+        sems,
+    ) = refs[2 * chunks - 2 :]
     rows = q_ref.shape[0]
     span = chunks * rows
     shared = own_key.shape[1] // HD
     loads = [
-        pltpu.make_async_copy(key_hbm, own_key, sems.at[0]),
-        pltpu.make_async_copy(value_hbm, own_value, sems.at[1]),
+        pltpu.make_async_copy(lengths_hbm, lengths_ref, sems.at[0]),
+        pltpu.make_async_copy(key_hbm, own_key, sems.at[1]),
+        pltpu.make_async_copy(value_hbm, own_value, sems.at[2]),
     ]
     for kv in range(shared):
         at = head(kv * group, group)
-        loads.append(pltpu.make_async_copy(q_hbm.at[:, at], q_ref.at[:, at], sems.at[2 + kv]))
+        loads.append(pltpu.make_async_copy(q_hbm.at[:, at], q_ref.at[:, at], sems.at[3 + kv]))
     for load in loads:
         load.start()
+    value_ref[:, HD:] = jnp.ones((span, HD), value_ref.dtype)
+    loads[0].wait()
     bias = mask_bias(lengths_ref, rows, span + rows)
     far_bias_ref[...] = bias[:, :rows]
-    bias = jnp.concatenate([bias[:, rows:]] * STACK, axis=0)
-    value_ref[:, HD:] = jnp.ones((span, HD), value_ref.dtype)
-    loads[0].wait()
+    bias = jnp.concatenate([bias[:, rows:]] * NEAR_STACK, axis=0)
     loads[1].wait()
+    loads[2].wait()
     for kv in range(shared):
         keys = jnp.concatenate([ref[:, head(kv)] for ref in (*key_refs, own_key)], axis=0)
         for i, ref in enumerate((*value_refs, own_value)):
             value_ref[i * rows : (i + 1) * rows, :HD] = ref[:, head(kv)]
         values = value_ref[...]
-        loads[2 + kv].wait()
-        for first in range(kv * group, (kv + 1) * group, STACK):
-            columns = [head(first + i) for i in range(STACK)]
+        loads[3 + kv].wait()
+        for first in range(kv * group, (kv + 1) * group, NEAR_STACK):
+            columns = [head(first + i) for i in range(NEAR_STACK)]
             scores = lax.dot_general(
                 row_stack(q_ref, columns),
                 keys,
@@ -95,7 +109,7 @@
             row_max = jnp.max(scores, axis=1, keepdims=True)
             weights = jnp.exp2((scores - row_max) * exp2_scale).astype(BF16)
             mixed = jnp.dot(weights, values, preferred_element_type=F32)
-            row_max = jnp.broadcast_to(row_max, (STACK * rows, HD))
+            row_max = jnp.broadcast_to(row_max, (NEAR_STACK * rows, HD))
             for i, at in enumerate(columns):
                 part = slice(i * rows, (i + 1) * rows)
                 max_ref[:, at] = row_max[part]
@@ -112,11 +126,11 @@
     return scratch[...]
 
 
-def head_pairs(shared, group):
+def head_pairs(shared, group, stack):
     for a in range(0, shared, 2):
-        for first in range(0, group, STACK):
-            yield a, [
-                [head((a + side) * group + first + i) for i in range(STACK)] for side in range(2)
+        for first in range(0, group, stack):
+            yield a, first, [
+                [head((a + side) * group + first + i) for i in range(stack)] for side in range(2)
             ]
 
 
@@ -136,12 +150,12 @@
     return jnp.concatenate([jnp.broadcast_to(p, (block.shape[0], HD)) for p in parts], axis=1)
 
 
-def far_kernel(group, q_ref, key_ref, bias_ref, max_ref, sum_ref, mixed_ref, weight_ref, scale_ref, faded_ref, pair_ref):
+def far_kernel(group, q_ref, key_ref, bias_ref, max_ref, sum_ref, mixed_ref, weight_ref, total_ref, faded_ref, pair_ref):
     shared = key_ref.shape[1] // HD
-    bias = jnp.concatenate([bias_ref[...]] * STACK, axis=0)
+    bias = jnp.concatenate([bias_ref[...]] * FAR_STACK, axis=0)
     bias = jnp.concatenate([bias] * 2, axis=1)
     done = None
-    for a, columns in head_pairs(shared, group):
+    for a, _, columns in head_pairs(shared, group, FAR_STACK):
         if a != done:
             keys = block_diagonal(key_ref[:, head(a)], key_ref[:, head(a + 1)], pair_ref)
             done = a
@@ -153,27 +167,30 @@
         new_max = jnp.maximum(old_max, per_side(jnp.max, scores))
         weights = jnp.exp2((scores - new_max) * exp2_scale)
         fade = jnp.exp2((old_max - new_max) * exp2_scale)
-        scale = 1.0 / (side_by_side(sum_ref, columns) * fade + per_side(jnp.sum, weights))
+        total = side_by_side(sum_ref, columns) * fade + per_side(jnp.sum, weights)
         put_pair(weight_ref, columns, weights.astype(BF16))
-        put_pair(scale_ref, columns, scale)
-        put_pair(faded_ref, columns, side_by_side(mixed_ref, columns) * (fade * scale))
-
-
-def last_kernel(group, value_ref, relay_ref, weight_ref, scale_ref, faded_ref, out_ref, pair_ref, staged_ref, sems):
+        put_pair(total_ref, columns, total)
+        put_pair(faded_ref, columns, side_by_side(mixed_ref, columns) * fade)
+
+
+def last_kernel(group, value_ref, relay_ref, weight_ref, total_ref, faded_ref, out_ref, pair_ref, staged_ref, sems):
     shared = value_ref.shape[1] // HD
     copies = []
     done = None
-    for a, columns in head_pairs(shared, group):
+    for a, first, columns in head_pairs(shared, group, LAST_STACK):
         if a != done:
             values = block_diagonal(
                 *[value_ref[:, head(kv)] + relay_ref[:, head(kv)] for kv in (a, a + 1)], pair_ref
             )
             done = a
         mixed = jnp.dot(side_by_side(weight_ref, columns), values, preferred_element_type=F32)
-        mixed = side_by_side(faded_ref, columns) + mixed * side_by_side(scale_ref, columns)
+        mixed = (side_by_side(faded_ref, columns) + mixed) / side_by_side(total_ref, columns)
         put_pair(staged_ref, columns, mixed.astype(staged_ref.dtype))
-        for side in columns:
-            at = slice(side[0].start, side[-1].stop)
+        ready = first + LAST_STACK
+        if ready % PIECE:
+            continue
+        for kv in (a, a + 1):
+            at = head(kv * group + ready - PIECE, PIECE)
             copies.append(
                 pltpu.make_async_copy(
                     staged_ref.at[:, at], out_ref.at[:, at], sems.at[len(copies)]
@@ -209,14 +226,15 @@
     *near_values, own_values = near_values
     queries, row_max, row_sum, mixed, far_bias = pl.pallas_call(
         functools.partial(near_kernel, chunks, group),
-        in_specs=[pl.BlockSpec(memory_space=pltpu.SMEM)] + [outside] * 3 + [whole] * (2 * chunks - 2),
+        in_specs=[outside] * 4 + [whole] * (2 * chunks - 2),
         out_specs=[whole] * 5,
         out_shape=[narrow, wide, wide, wide, pltpu.VMEM((rows, rows), F32)],
         scratch_shapes=[
+            pltpu.SMEM(seq_lengths.shape, seq_lengths.dtype),
             own,
             own,
             pltpu.VMEM((chunks * rows, 2 * HD), BF16),
-            pltpu.SemaphoreType.DMA((2 + shared,)),
+            pltpu.SemaphoreType.DMA((3 + shared,)),
         ],
         compiler_params=params,
         cost_estimate=pl.CostEstimate(
@@ -228,7 +246,7 @@
         *map(on_chip, near_keys),
         *map(on_chip, near_values),
     )
-    weights, scale, faded = pl.pallas_call(
+    weights, total, faded = pl.pallas_call(
         functools.partial(far_kernel, group),
         in_specs=[whole] * 6,
         out_specs=[whole] * 3,
@@ -240,7 +258,7 @@
         ),
         name="far",
     )(queries, on_chip(far_keys), far_bias, row_max, row_sum, mixed)
-    copies = 2 * (shared // 2) * (group // STACK)
+    copies = shared * (group // PIECE)
     return pl.pallas_call(
         functools.partial(last_kernel, group),
         in_specs=[whole] * 5,
@@ -249,7 +267,7 @@
         scratch_shapes=[pair, narrow, pltpu.SemaphoreType.DMA((copies,))],
         compiler_params=params,
         name="last",
-    )(on_chip(far_values), on_chip(relayed), weights, scale, faded)
+    )(on_chip(far_values), on_chip(relayed), weights, total, faded)
 
 
 def body(queries, key_proj, value_proj, seq_lengths):

time: 24.8 us -> 23.8 us (0.960)
  the two profiles are of different devices: /device:TPU:1 before, /device:TPU:4 now
where the time goes in v4:
time: 23.8 us; the launch traced here: 23.6 us
  starting transfers between devices  13.9 us (58%)
  Pallas kernels  6.64 us (28%)
  waiting for transfers between devices  2.97 us (12%)
    ppermute x5, starting transfers between devices, shift(): lax.ppermute(block, AXES, [(t - distance, t) for t in range(distance, cou...  13.9 us
    pallas_call x1, Pallas kernels, attend(): pl.pallas_call(functools.partial(near_kernel, chunks, group), in_specs=[o...  3.67 us
    ppermute x5, waiting for transfers between devices, shift(): lax.ppermute(block, AXES, [(t - distance, t) for t in range(distance, cou...  2.97 us
    pallas_call x1, Pallas kernels, attend(): pl.pallas_call(functools.partial(far_kernel, group), in_specs=[whole] * 6...  1.63 us
    pallas_call x1, Pallas kernels, attend(): pl.pallas_call(functools.partial(last_kernel, group), in_specs=[whole] *...  1.34 us
  transfers between devices with their start and end apart: 5, of which 2 were waited for; matrix products, arithmetic and copies ran while one was open for 0% of the time, Pallas kernels for 22%

profile of v4, /device:TPU:4, one launch (start us, length us, event | category | flops | bytes accessed | tf_op | source)
XLA Modules:
  0.0 23.6 jit_solution(6856292792555940132)
XLA Ops:
  0.0 3.5 %collective-permute-start.1 = (bf16[128,512]{1,0:T(8,128)(2,1)}, bf16[128,512]{1,0:T(8,128)(2,1)S(1)}, u32[]{:S(2)}, u32[]{:S(2)}) collective-permute-start(bf16[128,512]{1,0:T(8,128)(2,1)} %value_hbm.1), channel_id=1, source_target_pairs={{0,1},{1,2},{2,3},{3,4},{4,5},{5,6},{6,7},{7,8},{8,9},{9,10},{10,1... | collective-permute-start | bytes 393224 | tf_op jit(solution)/shard_map/ppermute | solution.py:29
  3.5 3.5 %collective-permute-start.3 = (bf16[128,512]{1,0:T(8,128)(2,1)}, bf16[128,512]{1,0:T(8,128)(2,1)S(1)}, u32[]{:S(2)}, u32[]{:S(2)}) collective-permute-start(bf16[128,512]{1,0:T(8,128)(2,1)} %key_hbm.1), channel_id=1, source_target_pairs={{0,1},{1,2},{2,3},{3,4},{4,5},{5,6},{6,7},{7,8},{8,9},{9,10},{10,1... | collective-permute-start | bytes 393224 | tf_op jit(solution)/shard_map/ppermute | solution.py:29
  7.0 2.9 %collective-permute-start.4 = (bf16[128,512]{1,0:T(8,128)(2,1)}, bf16[128,512]{1,0:T(8,128)(2,1)S(1)}, u32[]{:S(2)}, u32[]{:S(2)}) collective-permute-start(bf16[128,512]{1,0:T(8,128)(2,1)} %key_hbm.1), channel_id=1, source_target_pairs={{0,2},{1,3},{2,4},{3,5},{4,6},{5,7},{6,8},{7,9},{8,10},{9,11},{10,... | collective-permute-start | bytes 393224 | tf_op jit(solution)/shard_map/ppermute | solution.py:29
  9.9 2.7 %collective-permute-start = (bf16[128,512]{1,0:T(8,128)(2,1)}, bf16[128,512]{1,0:T(8,128)(2,1)S(1)}, u32[]{:S(2)}, u32[]{:S(2)}) collective-permute-start(bf16[128,512]{1,0:T(8,128)(2,1)} %value_hbm.1), channel_id=1, source_target_pairs={{0,2},{2,4},{4,6},{6,8},{8,10},{10,12},{12,14},{14,16},{16,18},{18... | collective-permute-start | bytes 393224 | tf_op jit(solution)/shard_map/ppermute | solution.py:29
  12.6 0.0 collective-permute-done.1.refs_1_
  12.6 1.3 %collective-permute-start.2 = (bf16[128,512]{1,0:T(8,128)(2,1)S(1)}, bf16[128,512]{1,0:T(8,128)(2,1)S(1)}, u32[]{:S(2)}, u32[]{:S(2)}) collective-permute-start(bf16[128,512]{1,0:T(8,128)(2,1)S(1)} %collective-permute-done.1.refs_1_), channel_id=1, source_target_pairs={{2,3},{4,5},{6,7},{8,9},{10,11},{12,13},{14,15},{16,17},{18,19},{2... | collective-permute-start | bytes 393224 | tf_op jit(solution)/shard_map/ppermute | solution.py:29
  13.9 0.0 collective-permute-done.3.refs_0_
  13.9 3.7 %near.1 = (bf16[128,4096]{1,0:T(8,128)(2,1)S(1)}, f32[128,4096]{1,0:T(8,128)S(1)}, f32[128,4096]{1,0:T(8,128)S(1)}, f32[128,4096]{1,0:T(8,128)S(1)}, f32[128,128]{1,0:T(8,128)S(1)}) custom-call(s32[32]{0:T(128)} %lengths_hbm.1, bf16[128,4096]{1,0:T(8,128)(2,1)} %q_hbm.1, bf16[128,512]{1,0:T(8,128)(2,1)} %key_hbm.1, bf16[128,512]{1,0:T(8,128)(2,1)} %value_hbm.1, ...), custom_call_target="tpu_custom_call" | custom-call | flops 805306368 | bytes 7340032 | tf_op jit(solution)/shard_map/near/pallas_call | solution.py:227
  17.6 2.4 %collective-permute-done.4.key_ref = bf16[128,512]{1,0:T(8,128)(2,1)S(1)} collective-permute-done((bf16[128,512]{1,0:T(8,128)(2,1)}, bf16[128,512]{1,0:T(8,128)(2,1)S(1)}, u32[]{:S(2)}, u32[]{:S(2)}) %collective-permute-start.4) | collective-permute-done | bytes 131104 | tf_op jit(solution)/shard_map/ppermute | solution.py:29
  20.0 1.6 %far.1 = (bf16[128,4096]{1,0:T(8,128)(2,1)S(1)}, f32[128,4096]{1,0:T(8,128)S(1)}, f32[128,4096]{1,0:T(8,128)S(1)}) custom-call(bf16[128,4096]{1,0:T(8,128)(2,1)S(1)} %get-tuple-element.13.q_ref, bf16[128,512]{1,0:T(8,128)(2,1)S(1)} %collective-permute-done.4.key_ref, f32[128,128]{1,0:T(8,128)S(1)} %get-tuple-element.14.bias_ref, ...), custom_call_target="tpu_custom_call" | custom-call | flops 134217728 | bytes 12582912 | tf_op jit(solution)/shard_map/far/pallas_call | solution.py:249
  21.7 0.6 %collective-permute-done.value_ref = bf16[128,512]{1,0:T(8,128)(2,1)S(1)} collective-permute-done((bf16[128,512]{1,0:T(8,128)(2,1)}, bf16[128,512]{1,0:T(8,128)(2,1)S(1)}, u32[]{:S(2)}, u32[]{:S(2)}) %collective-permute-start) | collective-permute-done | bytes 131104 | tf_op jit(solution)/shard_map/ppermute | solution.py:29
  22.2 0.0 collective-permute-done.2.relay_ref
  22.2 1.3 %last.1 = bf16[128,4096]{1,0:T(8,128)(2,1)} custom-call(bf16[128,512]{1,0:T(8,128)(2,1)S(1)} %collective-permute-done.value_ref, bf16[128,512]{1,0:T(8,128)(2,1)S(1)} %collective-permute-done.2.relay_ref, bf16[128,4096]{1,0:T(8,128)(2,1)S(1)} %get-tuple-element.18.weight_ref, f32[128,4096]{1,0:T(8,128)S(1)} %get-tuple-element.19.total_ref, ...), custom_call_target="tpu_custom_call" | custom-call | tf_op jit(solution)/shard_map/last/pallas_call | solution.py:262
Async XLA Ops:
  0.0 12.6 %collective-permute-start.1 = (bf16[128,512]{1,0:T(8,128)(2,1)}, bf16[128,512]{1,0:T(8,128)(2,1)S(1)}, u32[]{:S(2)}, u32[]{:S(2)}) collective-permute-start(bf16[128,512]{1,0:T(8,128)(2,1)} %value_hbm.1), channel_id=1, source_target_pairs={{0,1},{1,2},{2,3},{3,4},{4,5},{5,6},{6,7},{7,8},{8,9},{9,10},{10,1... | collective-permute-start | bytes 393224 | tf_op jit(solution)/shard_map/ppermute | solution.py:29
  3.5 10.4 %collective-permute-start.3 = (bf16[128,512]{1,0:T(8,128)(2,1)}, bf16[128,512]{1,0:T(8,128)(2,1)S(1)}, u32[]{:S(2)}, u32[]{:S(2)}) collective-permute-start(bf16[128,512]{1,0:T(8,128)(2,1)} %key_hbm.1), channel_id=1, source_target_pairs={{0,1},{1,2},{2,3},{3,4},{4,5},{5,6},{6,7},{7,8},{8,9},{9,10},{10,1... | collective-permute-start | bytes 393224 | tf_op jit(solution)/shard_map/ppermute | solution.py:29
  7.0 13.0 %collective-permute-start.4 = (bf16[128,512]{1,0:T(8,128)(2,1)}, bf16[128,512]{1,0:T(8,128)(2,1)S(1)}, u32[]{:S(2)}, u32[]{:S(2)}) collective-permute-start(bf16[128,512]{1,0:T(8,128)(2,1)} %key_hbm.1), channel_id=1, source_target_pairs={{0,2},{1,3},{2,4},{3,5},{4,6},{5,7},{6,8},{7,9},{8,10},{9,11},{10,... | collective-permute-start | bytes 393224 | tf_op jit(solution)/shard_map/ppermute | solution.py:29
  9.9 12.3 %collective-permute-start = (bf16[128,512]{1,0:T(8,128)(2,1)}, bf16[128,512]{1,0:T(8,128)(2,1)S(1)}, u32[]{:S(2)}, u32[]{:S(2)}) collective-permute-start(bf16[128,512]{1,0:T(8,128)(2,1)} %value_hbm.1), channel_id=1, source_target_pairs={{0,2},{2,4},{4,6},{6,8},{8,10},{10,12},{12,14},{14,16},{16,18},{18... | collective-permute-start | bytes 393224 | tf_op jit(solution)/shard_map/ppermute | solution.py:29
  12.6 9.6 %collective-permute-start.2 = (bf16[128,512]{1,0:T(8,128)(2,1)S(1)}, bf16[128,512]{1,0:T(8,128)(2,1)S(1)}, u32[]{:S(2)}, u32[]{:S(2)}) collective-permute-start(bf16[128,512]{1,0:T(8,128)(2,1)S(1)} %collective-permute-done.1.refs_1_), channel_id=1, source_target_pairs={{2,3},{4,5},{6,7},{8,9},{10,11},{12,13},{14,15},{16,17},{18,19},{2... | collective-permute-start | bytes 393224 | tf_op jit(solution)/shard_map/ppermute | solution.py:29

commit v5 on v4

v5 whole, which is shorter than its diff:
```python
import functools
import math

import jax
import jax.numpy as jnp
from jax import lax
from jax.experimental import pallas as pl
from jax.experimental.pallas import tpu as pltpu
from jax.sharding import PartitionSpec as P


HD = 128
NEAR_STACK = 2
FAR_STACK = 2
LAST_STACK = 2
PIECE = 8
EARLY_MEMBERS = lambda members: members // 2
PARTS = 1
VMEM_LIMIT = 24 << 20

AXES = ("dp", "seq")
score_scale = 0.08838834764831845
neg_fill = -1e30
exp2_scale = score_scale * math.log2(math.e)

F32 = jnp.float32
BF16 = jnp.bfloat16


def shift(block, distance, keep=lambda target: True):
    count = lax.axis_size(AXES)
    return lax.ppermute(block, AXES, [(t - distance, t) for t in range(distance, count) if keep(t)])


def head(index, count=1):
    return slice(index * HD, (index + count) * HD)


def row_stack(ref, columns):
    return jnp.concatenate([ref[:, at] for at in columns], axis=0)


def mask_bias(lengths_ref, rows, span):
    first = lax.axis_index(AXES) * rows
    key_pos = lax.broadcasted_iota(jnp.int32, (8, span), 1) + (first - span + rows)

    def step(i, carry):
        end, last = carry
        end = end + lengths_ref[i]
        return end, jnp.where(key_pos < end, jnp.minimum(last, end - 1), last)

    top = jnp.full((8, span), jnp.iinfo(jnp.int32).max, jnp.int32)
    _, last = lax.fori_loop(0, lengths_ref.shape[0], step, (jnp.int32(0), top), unroll=4)
    last = jnp.where(key_pos < 0, -1, last)
    query_pos = lax.broadcasted_iota(jnp.int32, (rows, span), 0) + first
    allowed = (query_pos >= key_pos[:1]) & (query_pos <= last[:1])
    return jnp.where(allowed, 0.0, neg_fill)


def load_kernel(early, lengths_hbm, q_hbm, key_hbm, value_hbm, *refs):
    is_early = lax.axis_index("seq") < EARLY_MEMBERS(lax.axis_size("seq"))
    pl.when(is_early if early else jnp.logical_not(is_early))(
        functools.partial(load_now, lengths_hbm, q_hbm, key_hbm, value_hbm, *refs[-7:])
    )


def load_now(lengths_hbm, q_hbm, key_hbm, value_hbm, *refs):
    q_ref, key_ref, value_ref, far_bias_ref, near_bias_ref, lengths_ref, sems = refs
    rows = q_ref.shape[0]
    span = near_bias_ref.shape[1]
    loads = [
        pltpu.make_async_copy(source, target, sems.at[i])
        for i, (source, target) in enumerate(
            (
                (lengths_hbm, lengths_ref),
                (q_hbm, q_ref),
                (key_hbm, key_ref),
                (value_hbm, value_ref),
            )
        )
    ]
    for load in loads:
        load.start()
    loads[0].wait()
    bias = mask_bias(lengths_ref, rows, span + rows)
    far_bias_ref[...] = bias[:, :rows]
    near_bias_ref[...] = bias[:, rows:]
    for load in loads[1:]:
        load.wait()


def near_kernel(chunks, group, q_ref, bias_ref, *refs):
    key_refs = refs[:chunks]
    value_refs = refs[chunks : 2 * chunks]
    max_ref, sum_ref, mixed_ref, value_ref = refs[2 * chunks :]
    rows = q_ref.shape[0]
    shared = key_refs[0].shape[1] // HD
    value_ref[:, HD:] = jnp.ones((chunks * rows, HD), value_ref.dtype)
    bias = jnp.concatenate([bias_ref[...]] * NEAR_STACK, axis=0)
    for kv in range(shared):
        keys = jnp.concatenate([ref[:, head(kv)] for ref in key_refs], axis=0)
        for i, ref in enumerate(value_refs):
            value_ref[i * rows : (i + 1) * rows, :HD] = ref[:, head(kv)]
        values = value_ref[...]
        for first in range(kv * group, (kv + 1) * group, NEAR_STACK):
            columns = [head(first + i) for i in range(NEAR_STACK)]
            scores = lax.dot_general(
                row_stack(q_ref, columns),
                keys,
                (((1,), (1,)), ((), ())),
                preferred_element_type=F32,
            )
            scores = scores + bias
            row_max = jnp.max(scores, axis=1, keepdims=True)
            weights = jnp.exp2((scores - row_max) * exp2_scale).astype(BF16)
            mixed = jnp.dot(weights, values, preferred_element_type=F32)
            row_max = jnp.broadcast_to(row_max, (NEAR_STACK * rows, HD))
            for i, at in enumerate(columns):
                part = slice(i * rows, (i + 1) * rows)
                max_ref[:, at] = row_max[part]
                mixed_ref[:, at] = mixed[part, :HD]
                sum_ref[:, at] = mixed[part, HD:]


def block_diagonal(first, second, scratch):
    rows = first.shape[0]
    scratch[:rows, :HD] = first
    scratch[rows:, HD:] = second
    scratch[:rows, HD:] = jnp.zeros((rows, HD), scratch.dtype)
    scratch[rows:, :HD] = jnp.zeros((rows, HD), scratch.dtype)
    return scratch[...]


def head_pairs(shared, group, stack):
    for a in range(0, shared, 2):
        for first in range(0, group, stack):
            yield a, first, [
                [head((a + side) * group + first + i) for i in range(stack)] for side in range(2)
            ]


def side_by_side(ref, part, columns):
    return jnp.concatenate(
        [jnp.concatenate([ref[part, at] for at in side], axis=0) for side in columns], axis=1
    )


def put_pair(ref, part, columns, block):
    rows = part.stop - part.start
    for side in range(2):
        for i, at in enumerate(columns[side]):
            ref[part, at] = block[i * rows : (i + 1) * rows, head(side)]


def per_side(reduce, block):
    parts = [reduce(block[:, head(side)], axis=1, keepdims=True) for side in range(2)]
    return jnp.concatenate([jnp.broadcast_to(p, (block.shape[0], HD)) for p in parts], axis=1)


def joined(refs, kv):
    return functools.reduce(jnp.add, [ref[:, head(kv)] for ref in refs])


def row_parts(bias_ref):
    size = bias_ref.shape[0] // PARTS
    for start in range(0, bias_ref.shape[0], size):
        yield slice(start, start + size), jnp.max(bias_ref[start : start + 8]) > neg_fill / 2


def far_kernel(pieces, group, *refs):
    key_refs = refs[:pieces]
    (
        q_ref,
        bias_ref,
        max_ref,
        sum_ref,
        mixed_ref,
        weight_ref,
        total_ref,
        faded_ref,
        pair_ref,
    ) = refs[pieces:]
    shared = key_refs[0].shape[1] // HD

    def merge(part):
        bias = jnp.concatenate([bias_ref[part]] * FAR_STACK, axis=0)
        bias = jnp.concatenate([bias] * 2, axis=1)
        for a, first, columns in head_pairs(shared, group, FAR_STACK):
            if first == 0:
                keys = block_diagonal(joined(key_refs, a), joined(key_refs, a + 1), pair_ref)
            scores = lax.dot_general(
                side_by_side(q_ref, part, columns),
                keys,
                (((1,), (1,)), ((), ())),
                preferred_element_type=F32,
            )
            scores = scores + bias
            old_max = side_by_side(max_ref, part, columns)
            new_max = jnp.maximum(old_max, per_side(jnp.max, scores))
            weights = jnp.exp2((scores - new_max) * exp2_scale)
            fade = jnp.exp2((old_max - new_max) * exp2_scale)
            total = side_by_side(sum_ref, part, columns) * fade + per_side(jnp.sum, weights)
            put_pair(weight_ref, part, columns, weights.astype(BF16))
            put_pair(total_ref, part, columns, total)
            put_pair(faded_ref, part, columns, side_by_side(mixed_ref, part, columns) * fade)

    for part, sees_far in row_parts(bias_ref):
        pl.when(sees_far)(functools.partial(merge, part))


def last_kernel(pieces, group, *refs):
    value_refs = refs[:pieces]
    (
        bias_ref,
        sum_ref,
        mixed_ref,
        weight_ref,
        total_ref,
        faded_ref,
        out_ref,
        pair_ref,
        staged_ref,
        sems,
    ) = refs[pieces:]
    shared = value_refs[0].shape[1] // HD
    parts = list(row_parts(bias_ref))

    def copy(index, part, kv, piece):
        at = head(kv * group + piece * PIECE, PIECE)
        number = (index * shared + kv) * (group // PIECE) + piece
        return pltpu.make_async_copy(
            staged_ref.at[part, at], out_ref.at[part, at], sems.at[number]
        )

    def finish(index, part, sees_far):
        for a, first, columns in head_pairs(shared, group, LAST_STACK):
            mixed = side_by_side(faded_ref if sees_far else mixed_ref, part, columns)
            if sees_far:
                if first == 0:
                    values = block_diagonal(
                        joined(value_refs, a), joined(value_refs, a + 1), pair_ref
                    )
                mixed = mixed + jnp.dot(
                    side_by_side(weight_ref, part, columns), values, preferred_element_type=F32
                )
            mixed = mixed / side_by_side(total_ref if sees_far else sum_ref, part, columns)
            put_pair(staged_ref, part, columns, mixed.astype(staged_ref.dtype))
            ready = first + LAST_STACK
            if ready % PIECE == 0:
                for kv in (a, a + 1):
                    copy(index, part, kv, ready // PIECE - 1).start()

    for index, (part, sees_far) in enumerate(parts):
        pl.when(sees_far)(functools.partial(finish, index, part, True))
        pl.when(jnp.logical_not(sees_far))(functools.partial(finish, index, part, False))
    for index, (part, _) in enumerate(parts):
        for kv in range(shared):
            for piece in range(group // PIECE):
                copy(index, part, kv, piece).wait()


def on_chip(array):
    return pltpu.with_memory_space_constraint(array, pltpu.VMEM)


def off_chip(array):
    return pltpu.with_memory_space_constraint(array, pltpu.HBM)


def attend(queries, near_keys, near_values, far_keys, far_values, seq_lengths):
    rows, width = queries.shape
    chunks = len(near_keys)
    shared = near_keys[0].shape[1] // HD
    group = width // near_keys[0].shape[1]
    whole = pl.BlockSpec(memory_space=pltpu.VMEM)
    outside = pl.BlockSpec(memory_space=pltpu.HBM)
    params = pltpu.CompilerParams(vmem_limit_bytes=VMEM_LIMIT)
    wide = pltpu.VMEM((rows, width), F32)
    narrow = pltpu.VMEM((rows, width), BF16)
    own = pltpu.VMEM(near_keys[0].shape, BF16)
    pair = pltpu.VMEM((2 * rows, 2 * HD), BF16)
    pairs = rows * width * rows
    *near_keys, own_keys = near_keys
    *near_values, own_values = near_values
    given = [off_chip(array) for array in (seq_lengths, queries, own_keys, own_values)]
    loaded = []
    for early in (True, False):
        loaded = pl.pallas_call(
            functools.partial(load_kernel, early),
            in_specs=[outside] * 4 + [whole] * len(loaded),
            out_specs=[whole] * 5,
            out_shape=[
                narrow,
                own,
                own,
                pltpu.VMEM((rows, rows), F32),
                pltpu.VMEM((rows, chunks * rows), F32),
            ],
            scratch_shapes=[
                pltpu.SMEM(seq_lengths.shape, seq_lengths.dtype),
                pltpu.SemaphoreType.DMA((4,)),
            ],
            input_output_aliases={4 + i: i for i in range(len(loaded))},
            compiler_params=params,
            name="early" if early else "load",
        )(*given, *loaded)
    queries, own_keys, own_values, far_bias, near_bias = loaded
    row_max, row_sum, mixed = pl.pallas_call(
        functools.partial(near_kernel, chunks, group),
        in_specs=[whole] * (2 + 2 * chunks),
        out_specs=[whole] * 3,
        out_shape=[wide, wide, wide],
        scratch_shapes=[pltpu.VMEM((chunks * rows, 2 * HD), BF16)],
        compiler_params=params,
        cost_estimate=pl.CostEstimate(
            flops=6 * chunks * pairs,
            transcendentals=chunks * pairs // HD,
            bytes_accessed=rows * width * 14,
        ),
        name="near",
    )(queries, near_bias, *map(on_chip, near_keys), own_keys, *map(on_chip, near_values), own_values)
    weights, total, faded = pl.pallas_call(
        functools.partial(far_kernel, len(far_keys), group),
        in_specs=[whole] * (5 + len(far_keys)),
        out_specs=[whole] * 3,
        out_shape=[narrow, wide, wide],
        scratch_shapes=[pair],
        compiler_params=params,
        cost_estimate=pl.CostEstimate(
            flops=2 * pairs, transcendentals=pairs // HD, bytes_accessed=rows * width * 24
        ),
        name="far",
    )(*map(on_chip, far_keys), queries, far_bias, row_max, row_sum, mixed)
    copies = PARTS * shared * (group // PIECE)
    return pl.pallas_call(
        functools.partial(last_kernel, len(far_values), group),
        in_specs=[whole] * (6 + len(far_values)),
        out_specs=outside,
        out_shape=jax.ShapeDtypeStruct((rows, width), queries.dtype),
        scratch_shapes=[pair, narrow, pltpu.SemaphoreType.DMA((copies,))],
        compiler_params=params,
        name="last",
    )(*map(on_chip, far_values), far_bias, row_sum, mixed, weights, total, faded)


def plan(rows, members):
    behind = -(-(rows * members // 2) // rows)
    return behind, lambda t: t % members < behind


def body(queries, key_proj, value_proj, seq_lengths):
    rows = queries.shape[0]
    members = lax.axis_size("seq")
    behind, _ = plan(rows, members)
    near_keys, near_values = [key_proj], [value_proj]
    for distance in range(1, behind):
        near_keys.insert(0, shift(key_proj, distance))
        near_values.insert(0, shift(value_proj, distance))
    far_keys = [
        shift(key_proj, behind, lambda t: t % members != 1),
        shift(near_keys[0], 1, lambda t: t % members == 1 and t >= behind),
    ]
    far_values = [
        shift(value_proj, behind, lambda t: t % members == 0),
        shift(near_values[0], 1, lambda t: t % members > 0 and t >= behind),
    ]
    return attend(queries, near_keys, near_values, far_keys, far_values, seq_lengths)


def solution(mesh):
    return jax.shard_map(
        body,
        mesh=mesh,
        in_specs=(P(AXES, None), P(AXES, None), P(AXES, None), P()),
        out_specs=P(AXES, None),
        check_vma=False,
    )
```

time: 23.8 us -> 26 us (1.092)
  the two profiles are of different devices: /device:TPU:4 before, /device:TPU:12 now
where the time goes in v5:
time: 26 us; the launch traced here: 25.7 us
  starting transfers between devices  19.4 us (75%)
  Pallas kernels  6.17 us (24%)
    ppermute x6, starting transfers between devices, shift(): lax.ppermute(block, AXES, [(t - distance, t) for t in range(distance, cou...  19.4 us
    pallas_call x1, Pallas kernels, attend(): pl.pallas_call(functools.partial(far_kernel, len(far_keys), group), in_sp...  1.76 us
    pallas_call x1, Pallas kernels, attend(): pl.pallas_call(functools.partial(near_kernel, chunks, group), in_specs=[w...  1.54 us
    pallas_call x1, Pallas kernels, attend(): pl.pallas_call(functools.partial(last_kernel, len(far_values), group), in...  1.51 us
    pallas_call x2, Pallas kernels, attend(): pl.pallas_call(functools.partial(load_kernel, early), in_specs=[outside]...  1.36 us
  transfers between devices with their start and end apart: 6, of which 0 were waited for; matrix products, arithmetic and copies ran while one was open for 0% of the time, Pallas kernels for 18%

profile of v5, /device:TPU:12, one launch (start us, length us, event | category | flops | bytes accessed | tf_op | source)
XLA Modules:
  0.0 25.7 jit_solution(892661010749067882)
XLA Ops:
  0.0 3.5 %collective-permute-start.3 = (bf16[128,512]{1,0:T(8,128)(2,1)}, bf16[128,512]{1,0:T(8,128)(2,1)S(1)}, u32[]{:S(2)}, u32[]{:S(2)}) collective-permute-start(bf16[128,512]{1,0:T(8,128)(2,1)} %key_hbm.3), channel_id=1, source_target_pairs={{0,1},{1,2},{2,3},{3,4},{4,5},{5,6},{6,7},{7,8},{8,9},{9,10},{10,1... | collective-permute-start | bytes 393224 | tf_op jit(solution)/shard_map/ppermute | solution.py:32
  3.5 3.5 %collective-permute-start.1 = (bf16[128,512]{1,0:T(8,128)(2,1)}, bf16[128,512]{1,0:T(8,128)(2,1)S(1)}, u32[]{:S(2)}, u32[]{:S(2)}) collective-permute-start(bf16[128,512]{1,0:T(8,128)(2,1)} %value_hbm.3), channel_id=1, source_target_pairs={{0,1},{1,2},{2,3},{3,4},{4,5},{5,6},{6,7},{7,8},{8,9},{9,10},{10,1... | collective-permute-start | bytes 393224 | tf_op jit(solution)/shard_map/ppermute | solution.py:32
  7.0 2.3 %collective-permute-start.4 = (bf16[128,512]{1,0:T(8,128)(2,1)}, bf16[128,512]{1,0:T(8,128)(2,1)S(1)}, u32[]{:S(2)}, u32[]{:S(2)}) collective-permute-start(bf16[128,512]{1,0:T(8,128)(2,1)} %key_hbm.3), channel_id=1, source_target_pairs={{0,2},{1,3},{2,4},{4,6},{5,7},{6,8},{8,10},{9,11},{10,12},{12,14},... | collective-permute-start | bytes 393224 | tf_op jit(solution)/shard_map/ppermute | solution.py:32
  9.3 0.0 collective-permute-done.3.refs_0_
  9.3 1.3 %collective-permute-start.5 = (bf16[128,512]{1,0:T(8,128)(2,1)S(1)}, bf16[128,512]{1,0:T(8,128)(2,1)S(1)}, u32[]{:S(2)}, u32[]{:S(2)}) collective-permute-start(bf16[128,512]{1,0:T(8,128)(2,1)S(1)} %collective-permute-done.3.refs_0_), channel_id=1, source_target_pairs={{4,5},{8,9},{12,13},{16,17},{20,21},{24,25},{28,29}} | collective-permute-start | bytes 393224 | tf_op jit(solution)/shard_map/ppermute | solution.py:32
  10.6 0.7 %collective-permute-start = (bf16[128,512]{1,0:T(8,128)(2,1)}, bf16[128,512]{1,0:T(8,128)(2,1)S(1)}, u32[]{:S(2)}, u32[]{:S(2)}) collective-permute-start(bf16[128,512]{1,0:T(8,128)(2,1)} %value_hbm.3), channel_id=1, source_target_pairs={{2,4},{6,8},{10,12},{14,16},{18,20},{22,24},{26,28}} | collective-permute-start | bytes 393224 | tf_op jit(solution)/shard_map/ppermute | solution.py:32
  11.3 0.0 collective-permute-done.1.refs_2_
  11.3 8.2 %collective-permute-start.2 = (bf16[128,512]{1,0:T(8,128)(2,1)S(1)}, bf16[128,512]{1,0:T(8,128)(2,1)S(1)}, u32[]{:S(2)}, u32[]{:S(2)}) collective-permute-start(bf16[128,512]{1,0:T(8,128)(2,1)S(1)} %collective-permute-done.1.refs_2_), channel_id=1, source_target_pairs={{1,2},{2,3},{4,5},{5,6},{6,7},{8,9},{9,10},{10,11},{12,13},{13,14}... | collective-permute-start | bytes 393224 | tf_op jit(solution)/shard_map/ppermute | solution.py:32
  19.5 1.3 %early.1 = (bf16[128,4096]{1,0:T(8,128)(2,1)S(1)}, bf16[128,512]{1,0:T(8,128)(2,1)S(1)}, bf16[128,512]{1,0:T(8,128)(2,1)S(1)}, f32[128,128]{1,0:T(8,128)S(1)}, f32[128,256]{1,0:T(8,128)S(1)}) custom-call(s32[32]{0:T(128)} %lengths_hbm.3, bf16[128,4096]{1,0:T(8,128)(2,1)} %q_hbm.3, bf16[128,512]{1,0:T(8,128)(2,1)} %key_hbm.3, bf16[128,512]{1,0:T(8,128)(2,1)} %value_hbm.3), custom_call_target="tpu_custom_call" | custom-call | tf_op jit(solution)/shard_map/early/pallas_call | solution.py:288
  20.8 0.1 load.1
  20.9 1.5 %near.1 = (f32[128,4096]{1,0:T(8,128)S(1)}, f32[128,4096]{1,0:T(8,128)S(1)}, f32[128,4096]{1,0:T(8,128)S(1)}) custom-call(bf16[128,4096]{1,0:T(8,128)(2,1)S(1)} %get-tuple-element.27.q_ref.refs_2_, f32[128,256]{1,0:T(8,128)S(1)} %get-tuple-element.28.bias_ref, bf16[128,512]{1,0:T(8,128)(2,1)S(1)} %collective-permute-done.3.refs_0_, ...), custom_call_target="tpu_custom_call" | custom-call | flops 805306368 | bytes 7340032 | tf_op jit(solution)/shard_map/near/pallas_call | solution.py:308
  22.4 0.0 collective-permute-done.4.refs_0_
  22.4 0.0 collective-permute-done.5.refs_1_
  22.4 1.8 %far.1 = (bf16[128,4096]{1,0:T(8,128)(2,1)S(1)}, f32[128,4096]{1,0:T(8,128)S(1)}, f32[128,4096]{1,0:T(8,128)S(1)}) custom-call(bf16[128,512]{1,0:T(8,128)(2,1)S(1)} %collective-permute-done.4.refs_0_, bf16[128,512]{1,0:T(8,128)(2,1)S(1)} %collective-permute-done.5.refs_1_, bf16[128,4096]{1,0:T(8,128)(2,1)S(1)} %get-tuple-element.27.q_ref.refs_2_, ...), custom_call_target="tpu_custom_call" | custom-call | flops 134217728 | bytes 12582912 | tf_op jit(solution)/shard_map/far/pallas_call | solution.py:322
  24.2 0.0 collective-permute-done.refs_0_
  24.2 0.0 collective-permute-done.2.refs_1_
  24.2 1.5 %last.1 = bf16[128,4096]{1,0:T(8,128)(2,1)} custom-call(bf16[128,512]{1,0:T(8,128)(2,1)S(1)} %collective-permute-done.refs_0_, bf16[128,512]{1,0:T(8,128)(2,1)S(1)} %collective-permute-done.2.refs_1_, f32[128,128]{1,0:T(8,128)S(1)} %get-tuple-element.26.refs_3_.refs_2_, f32[128,4096]{1,0:T(8,128)S(1)} %get-tuple-element.31.refs_5_.refs_3_, ...), custom_call_target="tpu_custom_call" | custom-call | tf_op jit(solution)/shard_map/last/pallas_call | solution.py:335
Async XLA Ops:
  0.0 9.3 %collective-permute-start.3 = (bf16[128,512]{1,0:T(8,128)(2,1)}, bf16[128,512]{1,0:T(8,128)(2,1)S(1)}, u32[]{:S(2)}, u32[]{:S(2)}) collective-permute-start(bf16[128,512]{1,0:T(8,128)(2,1)} %key_hbm.3), channel_id=1, source_target_pairs={{0,1},{1,2},{2,3},{3,4},{4,5},{5,6},{6,7},{7,8},{8,9},{9,10},{10,1... | collective-permute-start | bytes 393224 | tf_op jit(solution)/shard_map/ppermute | solution.py:32
  3.5 7.8 %collective-permute-start.1 = (bf16[128,512]{1,0:T(8,128)(2,1)}, bf16[128,512]{1,0:T(8,128)(2,1)S(1)}, u32[]{:S(2)}, u32[]{:S(2)}) collective-permute-start(bf16[128,512]{1,0:T(8,128)(2,1)} %value_hbm.3), channel_id=1, source_target_pairs={{0,1},{1,2},{2,3},{3,4},{4,5},{5,6},{6,7},{7,8},{8,9},{9,10},{10,1... | collective-permute-start | bytes 393224 | tf_op jit(solution)/shard_map/ppermute | solution.py:32
  7.0 15.4 %collective-permute-start.4 = (bf16[128,512]{1,0:T(8,128)(2,1)}, bf16[128,512]{1,0:T(8,128)(2,1)S(1)}, u32[]{:S(2)}, u32[]{:S(2)}) collective-permute-start(bf16[128,512]{1,0:T(8,128)(2,1)} %key_hbm.3), channel_id=1, source_target_pairs={{0,2},{1,3},{2,4},{4,6},{5,7},{6,8},{8,10},{9,11},{10,12},{12,14},... | collective-permute-start | bytes 393224 | tf_op jit(solution)/shard_map/ppermute | solution.py:32
  9.3 13.1 %collective-permute-start.5 = (bf16[128,512]{1,0:T(8,128)(2,1)S(1)}, bf16[128,512]{1,0:T(8,128)(2,1)S(1)}, u32[]{:S(2)}, u32[]{:S(2)}) collective-permute-start(bf16[128,512]{1,0:T(8,128)(2,1)S(1)} %collective-permute-done.3.refs_0_), channel_id=1, source_target_pairs={{4,5},{8,9},{12,13},{16,17},{20,21},{24,25},{28,29}} | collective-permute-start | bytes 393224 | tf_op jit(solution)/shard_map/ppermute | solution.py:32
  10.6 13.6 %collective-permute-start = (bf16[128,512]{1,0:T(8,128)(2,1)}, bf16[128,512]{1,0:T(8,128)(2,1)S(1)}, u32[]{:S(2)}, u32[]{:S(2)}) collective-permute-start(bf16[128,512]{1,0:T(8,128)(2,1)} %value_hbm.3), channel_id=1, source_target_pairs={{2,4},{6,8},{10,12},{14,16},{18,20},{22,24},{26,28}} | collective-permute-start | bytes 393224 | tf_op jit(solution)/shard_map/ppermute | solution.py:32
  11.3 12.9 %collective-permute-start.2 = (bf16[128,512]{1,0:T(8,128)(2,1)S(1)}, bf16[128,512]{1,0:T(8,128)(2,1)S(1)}, u32[]{:S(2)}, u32[]{:S(2)}) collective-permute-start(bf16[128,512]{1,0:T(8,128)(2,1)S(1)} %collective-permute-done.1.refs_2_), channel_id=1, source_target_pairs={{1,2},{2,3},{4,5},{5,6},{6,7},{8,9},{9,10},{10,11},{12,13},{13,14}... | collective-permute-start | bytes 393224 | tf_op jit(solution)/shard_map/ppermute | solution.py:32
